TPU v7x, 512 devices: a whole 4x8x8 slice. The times are simulated.
512 devices in a mesh: mid: 64 (over y, z), fin: 8 (over x, core).
Axes of the slice: x: 4, y: 8, z: 8, core: 2. Of those that a mesh axis runs over, the one named last changes fastest.
Arguments:
- history: float32 [1024, 64, 64, 128], P('mid', 'fin'), may hold values from -6 to 6
- sigma: float32 [4, 1024, 64, 128], P(None, 'mid', 'fin'), may hold values from -0.01171875 to 0.01171875
- propagator: float32 [64, 128], replicated, may hold values from -0.375 to 0.375
Outputs:
- new_rows: float32 [4, 64, 64, 128], P(None, 'fin', 'mid')
All inputs are finite; a program needn't handle non-finite values.
Results may differ from a plain program's by a relative error of at most 0.0003.
Values sent between devices are 32-bit elements; how exact they have to be, the bound alone decides.
No kernel may reach another device: no remote copies, remote signals or barrier semaphores. Data moves between devices by JAX's collectives and lax.ppermute only.
A program may use at most 128 MiB of HBM per device.

v0:
```python
import jax
import jax.numpy as jnp
from jax import lax
from jax.experimental import pallas as pl
from jax.experimental.pallas import tpu as pltpu
from jax.sharding import Mesh, PartitionSpec as P

STEPS = 4
PAIRS = [(k, l) for k in range(1, STEPS) for l in range(k)]
HIGHEST = lax.Precision.HIGHEST


def split(value):
    high = value.astype(jnp.bfloat16)
    low = (value - high.astype(jnp.float32)).astype(jnp.bfloat16)
    return high, low


def turn(block):
    lanes = block.shape[-1]
    half = lanes // 2
    rolled = pltpu.roll(block, half, block.ndim - 1)
    lane = lax.broadcasted_iota(jnp.int32, block.shape, block.ndim - 1)
    return jnp.where(lane < half, -rolled, rolled)


def memory_kernel(mid_ref, kernels_ref, history_ref, memory_ref, high_ref, low_ref):
    step = pl.program_id(0)
    sources, steps, parts, rows, depth = kernels_ref.shape
    lanes = history_ref.shape[-1]

    @pl.when(step == 0)
    def _():
        high, low = split(kernels_ref[...].reshape(sources * steps * parts * rows, depth))
        high_ref[...] = high
        low_ref[...] = low

    block = jnp.concatenate(
        [history_ref[:, c].reshape(depth, lanes) for c in range(2)], axis=1
    )
    block_high, block_low = split(block)
    dot = lambda a, b: jnp.dot(a, b, preferred_element_type=jnp.float32)
    total = dot(high_ref[...], block_high) + (
        dot(low_ref[...], block_high) + dot(high_ref[...], block_low)
    )
    total = total.reshape(sources, steps, parts, rows, 2 * lanes)
    for c in range(2):
        column = total[..., c * lanes : (c + 1) * lanes]
        value = column[:, :, 0] + turn(column[:, :, 1])
        kept = mid_ref[0] >= mid_ref[1] + 2 * step + c
        value = jnp.where(kept, value, 0.0)
        for k in range(steps):
            memory_ref[k, :, c * lanes : (c + 1) * lanes] = value[:, k].reshape(
                sources * rows, lanes
            )


def memory_terms(where, kernels, history):
    sources, steps, parts, rows, depth = kernels.shape
    slots, cols, orbitals, lanes = history.shape
    height = sources * steps * parts * rows
    return pl.pallas_call(
        memory_kernel,
        grid_spec=pltpu.PrefetchScalarGridSpec(
            num_scalar_prefetch=1,
            grid=(cols // 2,),
            in_specs=[
                pl.BlockSpec(kernels.shape, lambda g, w: (0, 0, 0, 0, 0)),
                pl.BlockSpec((slots, 2, orbitals, lanes), lambda g, w: (0, g, 0, 0)),
            ],
            out_specs=pl.BlockSpec((steps, orbitals, 2 * lanes), lambda g, w: (0, 0, g)),
            scratch_shapes=[pltpu.VMEM((height, depth), jnp.bfloat16)] * 2,
        ),
        out_shape=jax.ShapeDtypeStruct((steps, orbitals, cols * lanes), jnp.float32),
        compiler_params=pltpu.CompilerParams(dimension_semantics=("arbitrary",)),
        cost_estimate=pl.CostEstimate(
            flops=6 * height * depth * cols * lanes,
            bytes_accessed=8 << 20,
            transcendentals=0,
        ),
        name="memory_terms",
    )(where, kernels, history)


def recursion_kernel(memory_ref, blocks_ref, propagator_ref, out_ref):
    steps, orbitals, width = memory_ref.shape
    lanes = propagator_ref.shape[-1]
    cols = width // lanes
    stacked = []
    for k in range(steps):
        value = memory_ref[k]
        if k:
            weights = []
            for l in range(k):
                weight = blocks_ref[:, PAIRS.index((k, l))].reshape(orbitals, lanes)
                if l == k - 1:
                    weight = weight + propagator_ref[...]
                weights.append(weight)
            value = value + jnp.dot(
                jnp.concatenate(weights, axis=1),
                jnp.concatenate(stacked, axis=0),
                preferred_element_type=jnp.float32,
                precision=HIGHEST,
            )
        columns = [value[:, c * lanes : (c + 1) * lanes] for c in range(cols)]
        if k < steps - 1:
            stacked.append(value)
            stacked.append(jnp.concatenate([turn(column) for column in columns], axis=1))
        for c in range(cols):
            out_ref[:, k, c, :] = columns[c]


def recursion(memory, blocks, propagator):
    steps, orbitals, width = memory.shape
    lanes = propagator.shape[-1]
    return pl.pallas_call(
        recursion_kernel,
        out_shape=jax.ShapeDtypeStruct((orbitals, steps, width // lanes, lanes), jnp.float32),
        cost_estimate=pl.CostEstimate(
            flops=12 * 6 * orbitals * 2 * orbitals * width,
            bytes_accessed=3 << 20,
            transcendentals=0,
        ),
        name="recursion",
    )(memory, blocks, propagator)


def from_everyone(shard, axis):
    length = lax.axis_size(axis)
    return lax.all_to_all(
        jnp.broadcast_to(shard[None], (length, *shard.shape)), axis, 0, 0, tiled=True
    )


def on_device(history, sigma, propagator):
    mid_count = lax.axis_size(("y", "z"))
    fin_count = lax.axis_size(("x", "core"))
    mid_index = lax.axis_index(("y", "z"))
    fin_index = lax.axis_index(("x", "core"))
    slots, cols, orbitals, lanes = history.shape
    rows = sigma.shape[2]
    assert (mid_count * slots) // (fin_count * cols) == slots

    blocks = jnp.stack([sigma[k, l] for k, l in PAIRS])
    blocks = from_everyone(blocks, "z")[0]
    blocks = from_everyone(blocks, "y")[0]
    blocks = from_everyone(blocks, ("x", "core"))

    slot_ids = mid_index * slots + jnp.arange(slots, dtype=jnp.int32)
    steps = jnp.arange(STEPS, dtype=jnp.int32)
    old = slot_ids[None, :] >= steps[:, None]
    newest = (slot_ids[None, :] == mid_count * slots - 1) & (steps[:, None] == 0)
    own_rows = lax.dynamic_slice_in_dim(propagator, fin_index * rows, rows, 0)
    kernels = jnp.where(old[:, :, None, None], sigma, 0.0)
    kernels = kernels + jnp.where(newest[:, :, None, None], own_rows, 0.0)
    kernels = kernels.reshape(STEPS, slots, rows, 2, orbitals)
    kernels = kernels.transpose(0, 3, 2, 1, 4).reshape(STEPS, 2, rows, slots * orbitals)
    kernels = from_everyone(kernels, ("x", "core"))

    where = jnp.stack([mid_index, fin_index * cols]).astype(jnp.int32)
    memory = memory_terms(where, kernels, history)
    terms = recursion(memory, blocks, propagator)
    arrived = lax.all_to_all(terms, ("y", "z"), 0, 0, tiled=True)
    return arrived.sum(axis=0)[:, :, None, :]


def solution(mesh):
    devices = mesh.devices.reshape(8, 8, 4, 2)
    mesh = Mesh(devices, ("y", "z", "x", "core"))
    mid, fin = ("y", "z"), ("x", "core")
    in_specs = (P(mid, fin, None, None), P(None, mid, fin, None), P())
    out_specs = P(None, fin, mid, None)
    return jax.shard_map(
        on_device, mesh=mesh, in_specs=in_specs, out_specs=out_specs, check_vma=False
    )
```

profile of v0, /device:TPU:18, one launch (start us, length us, event | category | flops | bytes accessed | tf_op | source)
XLA Modules:
  0.0 130.4 jit_solution(13392579784793422303)
XLA Ops:
  0.0 0.7 constant_dynamic-update-slice_fusion.5
  0.7 0.7 constant_dynamic-update-slice_fusion.4
  1.4 0.7 constant_dynamic-update-slice_fusion.3
  2.1 0.7 constant_dynamic-update-slice_fusion.2
  2.8 0.7 constant_dynamic-update-slice_fusion.1
  3.4 0.7 constant_dynamic-update-slice_fusion
  4.1 0.7 broadcast_in_dim.68
  4.8 10.3 %all-to-all-start.1 = ((f32[8,6,8,128]{3,2,1,0:T(8,128)}), f32[8,6,8,128]{3,2,1,0:T(8,128)S(1)}, u32[]{:S(2)}, u32[]{:S(2)}) async-start(f32[8,6,8,128]{3,2,1,0:T(8,128)} %broadcast_in_dim.68), calls=%async_computation.1 | async-start | bytes 393216 | tf_op jit(solution)/shard_map/all_to_all | solution.py:130
  15.2 0.1 iota_compare_fusion
  15.3 10.3 %all-to-all-done.1 = f32[8,6,8,128]{3,2,1,0:T(8,128)S(1)} async-done(((f32[8,6,8,128]{3,2,1,0:T(8,128)}), f32[8,6,8,128]{3,2,1,0:T(8,128)S(1)}, u32[]{:S(2)}, u32[]{:S(2)}) %all-to-all-start.1) | async-done | bytes 196640 | tf_op jit(solution)/shard_map/all_to_all | solution.py:130
  25.6 0.7 broadcast_in_dim.70
  26.3 7.4 %all-to-all-start.2 = ((f32[8,6,8,128]{3,2,1,0:T(8,128)}), f32[8,6,8,128]{3,2,1,0:T(8,128)S(1)}, u32[]{:S(2)}, u32[]{:S(2)}) async-start(f32[8,6,8,128]{3,2,1,0:T(8,128)} %broadcast_in_dim.70), calls=%async_computation.2 | async-start | bytes 393216 | tf_op jit(solution)/shard_map/all_to_all | solution.py:130
  33.7 0.7 constant_dynamic-slice_fusion
  34.4 1.1 select_add_fusion
  35.6 0.3 reshape.64
  35.9 0.2 copy.4
  36.1 0.2 broadcast_in_dim.66
  36.2 4.8 %all-to-all-done.2 = f32[8,6,8,128]{3,2,1,0:T(8,128)S(1)} async-done(((f32[8,6,8,128]{3,2,1,0:T(8,128)}), f32[8,6,8,128]{3,2,1,0:T(8,128)S(1)}, u32[]{:S(2)}, u32[]{:S(2)}) %all-to-all-start.2) | async-done | bytes 196640 | tf_op jit(solution)/shard_map/all_to_all | solution.py:130
  41.1 1.6 %broadcast_in_dim.67 = f32[8,4,2,8,1024]{4,3,2,1,0:T(8,128)} broadcast(f32[4,2,8,1024]{3,2,1,0:T(8,128)S(1)} %broadcast_in_dim.66), dimensions={1,2,3,4} | broadcast | bytes 2359296 | tf_op jit(solution)/shard_map/broadcast_in_dim | solution.py:131
  42.7 4.8 %all-to-all-start = ((f32[8,4,2,8,1024]{4,3,2,1,0:T(8,128)}), f32[8,4,2,8,1024]{4,3,2,1,0:T(8,128)S(1)}, u32[]{:S(2)}, u32[]{:S(2)}) async-start(f32[8,4,2,8,1024]{4,3,2,1,0:T(8,128)} %broadcast_in_dim.67), calls=%async_computation | async-start | bytes 4194304 | tf_op jit(solution)/shard_map/all_to_all | solution.py:130
  47.5 0.7 pad_add_fusion.mid_ref
  48.2 25.0 %all-to-all-done.kernels_ref = f32[8,4,2,8,1024]{4,3,2,1,0:T(8,128)S(1)} async-done(((f32[8,4,2,8,1024]{4,3,2,1,0:T(8,128)}), f32[8,4,2,8,1024]{4,3,2,1,0:T(8,128)S(1)}, u32[]{:S(2)}, u32[]{:S(2)}) %all-to-all-start) | async-done | bytes 2097184 | tf_op jit(solution)/shard_map/all_to_all | solution.py:130
  73.2 0.0 copy-start
  73.2 0.7 broadcast_in_dim.72
  74.0 4.8 %all-to-all-start.3 = ((f32[8,6,8,128]{3,2,1,0:T(8,128)}), f32[8,6,8,128]{3,2,1,0:T(8,128)S(1)}, u32[]{:S(2)}, u32[]{:S(2)}) async-start(f32[8,6,8,128]{3,2,1,0:T(8,128)} %broadcast_in_dim.72), calls=%async_computation.3 | async-start | bytes 393216 | tf_op jit(solution)/shard_map/all_to_all | solution.py:130
  78.7 0.0 copy-done
  78.7 8.2 %memory_terms.1.memory_ref = f32[4,64,1024]{2,1,0:T(8,128)} custom-call(s32[2]{0:T(128)} %pad_add_fusion.mid_ref, f32[8,4,2,8,1024]{4,3,2,1,0:T(8,128)} %copy-done, f32[16,8,64,128]{3,2,1,0:T(8,128)} %history_ref.1), custom_call_target="tpu_custom_call" | custom-call | flops 3221225472 | bytes 8388608 | tf_op jit(solution)/shard_map/memory_terms/pallas_call | solution.py:62
  87.0 0.0 all-to-all-done.3.blocks_ref
  87.0 0.0 copy-start.1
  87.0 0.7 copy-done.1
  87.6 4.6 %recursion.1 = f32[64,4,8,128]{3,2,1,0:T(8,128)} custom-call(f32[4,64,1024]{2,1,0:T(8,128)} %memory_terms.1.memory_ref, f32[8,6,8,128]{3,2,1,0:T(8,128)} %copy-done.1, f32[64,128]{1,0:T(8,128)} %propagator_ref.1), custom_call_target="tpu_custom_call" | custom-call | flops 603979776 | bytes 3145728 | tf_op jit(solution)/shard_map/recursion/pallas_call | solution.py:116
  92.2 37.5 %all_to_all.25 = f32[64,4,8,128]{3,2,1,0:T(8,128)S(1)} all-to-all(f32[64,4,8,128]{3,2,1,0:T(8,128)} %recursion.1), channel_id=1, replica_groups=mesh['y'=8,'z'=8,'x'=4,'core'=2] {'y','z'}, dimensions={0} | all-to-all | bytes 2097152 | tf_op jit(solution)/shard_map/all_to_all | solution.py:163
  129.7 0.7 reduce_sum.9
  (5 shorter events, 0.0 us)
Async XLA Ops:
  4.8 20.8 %all-to-all-start.1 = ((f32[8,6,8,128]{3,2,1,0:T(8,128)}), f32[8,6,8,128]{3,2,1,0:T(8,128)S(1)}, u32[]{:S(2)}, u32[]{:S(2)}) async-start(f32[8,6,8,128]{3,2,1,0:T(8,128)} %broadcast_in_dim.68), calls=%async_computation.1 | async-start | bytes 393216 | tf_op jit(solution)/shard_map/all_to_all | solution.py:130
  26.3 14.8 %all-to-all-start.2 = ((f32[8,6,8,128]{3,2,1,0:T(8,128)}), f32[8,6,8,128]{3,2,1,0:T(8,128)S(1)}, u32[]{:S(2)}, u32[]{:S(2)}) async-start(f32[8,6,8,128]{3,2,1,0:T(8,128)} %broadcast_in_dim.70), calls=%async_computation.2 | async-start | bytes 393216 | tf_op jit(solution)/shard_map/all_to_all | solution.py:130
  42.7 30.5 %all-to-all-start = ((f32[8,4,2,8,1024]{4,3,2,1,0:T(8,128)}), f32[8,4,2,8,1024]{4,3,2,1,0:T(8,128)S(1)}, u32[]{:S(2)}, u32[]{:S(2)}) async-start(f32[8,4,2,8,1024]{4,3,2,1,0:T(8,128)} %broadcast_in_dim.67), calls=%async_computation | async-start | bytes 4194304 | tf_op jit(solution)/shard_map/all_to_all | solution.py:130
  73.2 5.5 %copy-start = (f32[8,4,2,8,1024]{4,3,2,1,0:T(8,128)}, f32[8,4,2,8,1024]{4,3,2,1,0:T(8,128)S(1)}, u32[]{:S(2)}) copy-start(f32[8,4,2,8,1024]{4,3,2,1,0:T(8,128)S(1)} %all-to-all-done.kernels_ref) | copy-start | bytes 6291460
  74.0 13.0 %all-to-all-start.3 = ((f32[8,6,8,128]{3,2,1,0:T(8,128)}), f32[8,6,8,128]{3,2,1,0:T(8,128)S(1)}, u32[]{:S(2)}, u32[]{:S(2)}) async-start(f32[8,6,8,128]{3,2,1,0:T(8,128)} %broadcast_in_dim.72), calls=%async_computation.3 | async-start | bytes 393216 | tf_op jit(solution)/shard_map/all_to_all | solution.py:130
  87.0 0.7 copy-start.1
where the time goes:
time: 131 us; the launch traced here: 130 us
  waiting for transfers between devices  40.2 us (31%)
  blocking collectives  37.5 us (29%)
  starting transfers between devices  27.3 us (21%)
  Pallas kernels  12.8 us (10%)
  local copies, waits for them, and re-layouts  9.84 us (8%)
  other arithmetic  2.61 us (2%)
    all_to_all x4, waiting for transfers between devices, from_everyone(): lax.all_to_all(jnp.broadcast_to(shard[None], (length, *shard.shape)), axi...  40.2 us
    all_to_all x1, blocking collectives, on_device(): arrived = lax.all_to_all(terms, ('y', 'z'), 0, 0, tiled=True)  37.5 us
    all_to_all x4, starting transfers between devices, from_everyone(): lax.all_to_all(jnp.broadcast_to(shard[None], (length, *shard.shape)), axi...  27.3 us
    pallas_call x1, Pallas kernels, memory_terms(): pl.pallas_call(memory_kernel, grid_spec=pltpu.PrefetchScalarGridSpec(num_...  8.24 us
    pallas_call x1, Pallas kernels, recursion(): pl.pallas_call(recursion_kernel, out_shape=jax.ShapeDtypeStruct((orbitals...  4.58 us
    unnamed x9, local copies, waits for them, and re-layouts  4.12 us
    broadcast_in_dim x7, local copies, waits for them, and re-layouts, from_everyone(): jnp.broadcast_to(shard[None], (length, *shard.shape))  3.87 us
  transfers between devices with their start and end apart: 4, of which 3 were waited for; matrix products, arithmetic and copies ran while one was open for 2% of the time, Pallas kernels for 6%

commit v1 on v0

v1 whole, which is shorter than its diff:
```python
import jax
import jax.numpy as jnp
from jax import lax
from jax.experimental import pallas as pl
from jax.experimental.pallas import tpu as pltpu
from jax.sharding import Mesh, PartitionSpec as P


STEPS = 4
AXES = ("y1", "y0", "z", "x", "core")
MID, FIN = AXES[:3], AXES[3:]
HIGHEST = lax.Precision.HIGHEST


def split(value):
    high = value.astype(jnp.bfloat16)
    low = (value - high.astype(jnp.float32)).astype(jnp.bfloat16)
    return high, low


def turn(block):
    lanes = block.shape[-1]
    half = lanes // 2
    rolled = pltpu.roll(block, half, block.ndim - 1)
    lane = lax.broadcasted_iota(jnp.int32, block.shape, block.ndim - 1)
    return jnp.where(lane < half, -rolled, rolled)


def memory_kernel(where_ref, sigma_ref, propagator_ref, history_ref, memory_ref, high_ref, low_ref):
    step = pl.program_id(0)
    sources, steps, slots, rows, lanes = sigma_ref.shape
    half = lanes // 2
    first_slot, mid_last, first_col, first_device, first_pair = (where_ref[n] for n in range(5))

    @pl.when(step == 0)
    def _():
        lane = lax.broadcasted_iota(jnp.int32, (rows, lanes), 1)
        for n in range(sources):
            own_rows = propagator_ref[n * rows : (n + 1) * rows, :]
            own_rows = jnp.where(mid_last == 1, own_rows, 0.0)
            for k in range(steps):
                for p in range(0, slots, 2):
                    pair = [sigma_ref[n, k, p], sigma_ref[n, k, p + 1]]
                    for q in range(2):
                        if p + q < k:
                            pair[q] = jnp.where(first_slot + p + q >= k, pair[q], 0.0)
                    if k == 0 and p + 2 == slots:
                        pair[1] = pair[1] + own_rows
                    real = jnp.where(lane < half, pair[0], pltpu.roll(pair[1], half, 1))
                    imag = jnp.where(lane < half, pltpu.roll(pair[0], half, 1), pair[1])
                    high, low = split(jnp.concatenate([real, imag], axis=0))
                    at = (
                        pl.ds((n * steps + k) * 2 * rows, 2 * rows),
                        pl.ds(p * half, lanes),
                    )
                    high_ref[at] = high
                    low_ref[at] = low

    depth = slots * half
    block = jnp.concatenate(
        [history_ref[:, c].reshape(depth, lanes) for c in range(2)], axis=1
    )
    block_high, block_low = split(block)
    dot = lambda a, b: jnp.dot(a, b, preferred_element_type=jnp.float32)
    total = dot(high_ref[...], block_high) + (
        dot(low_ref[...], block_high) + dot(high_ref[...], block_low)
    )
    total = total.reshape(sources, steps, 2, rows, 2 * lanes)
    for c in range(2):
        column = total[..., c * lanes : (c + 1) * lanes]
        value = column[:, :, 0] + turn(column[:, :, 1])
        kept = first_device >= first_col + 2 * (first_pair + step) + c
        value = jnp.where(kept, value, 0.0)
        for k in range(steps):
            memory_ref[c, k] = value[:, k].reshape(sources * rows, lanes)


def memory_terms(where, sigma, propagator, history, cols):
    sources, steps, _, rows, _ = sigma.shape
    slots, _, orbitals, lanes = history.shape
    height = sources * steps * 2 * rows
    depth = slots * orbitals
    whole = lambda array: pl.BlockSpec(array.shape, lambda g, w: (0,) * array.ndim)
    return pl.pallas_call(
        memory_kernel,
        grid_spec=pltpu.PrefetchScalarGridSpec(
            num_scalar_prefetch=1,
            grid=(cols // 2,),
            in_specs=[
                whole(sigma),
                whole(propagator),
                pl.BlockSpec((slots, 2, orbitals, lanes), lambda g, w: (0, w[4] + g, 0, 0)),
            ],
            out_specs=pl.BlockSpec((2, steps, orbitals, lanes), lambda g, w: (g, 0, 0, 0)),
            scratch_shapes=[pltpu.VMEM((height, depth), jnp.bfloat16)] * 2,
        ),
        out_shape=jax.ShapeDtypeStruct((cols, steps, orbitals, lanes), jnp.float32),
        compiler_params=pltpu.CompilerParams(dimension_semantics=("arbitrary",)),
        cost_estimate=pl.CostEstimate(
            flops=6 * height * depth * cols * lanes,
            bytes_accessed=6 << 20,
            transcendentals=0,
        ),
        name="memory_terms",
    )(where, sigma, propagator, history)


def recursion_kernel(own_ref, arrived_ref, blocks_ref, propagator_ref, out_ref):
    cols, steps, orbitals, lanes = own_ref.shape
    stacked = []
    for k in range(steps):
        columns = [own_ref[c, k] + arrived_ref[c, k] for c in range(cols)]
        if k:
            weights = []
            for l in range(k):
                weight = blocks_ref[:, k - 1, l].reshape(orbitals, lanes)
                if l == k - 1:
                    weight = weight + propagator_ref[...]
                weights.append(weight)
            update = jnp.dot(
                jnp.concatenate(weights, axis=1),
                jnp.concatenate(stacked, axis=0),
                preferred_element_type=jnp.float32,
                precision=HIGHEST,
            )
            columns = [
                columns[c] + update[:, c * lanes : (c + 1) * lanes] for c in range(cols)
            ]
        if k < steps - 1:
            stacked.append(jnp.concatenate(columns, axis=1))
            stacked.append(jnp.concatenate([turn(column) for column in columns], axis=1))
        for c in range(cols):
            out_ref[:, k * cols + c, :] = columns[c]


def recursion(own, arrived, blocks, propagator):
    cols, steps, orbitals, lanes = own.shape
    return pl.pallas_call(
        recursion_kernel,
        out_shape=jax.ShapeDtypeStruct((orbitals, steps * cols, lanes), jnp.float32),
        cost_estimate=pl.CostEstimate(
            flops=12 * 6 * orbitals * 2 * orbitals * cols * lanes,
            bytes_accessed=2 << 20,
            transcendentals=0,
        ),
        name="recursion",
    )(own, arrived, blocks, propagator)


def from_everyone(shard, axis):
    length = lax.axis_size(axis)
    return lax.all_to_all(
        jnp.broadcast_to(shard[None], (length, *shard.shape)), axis, 0, 0, tiled=True
    )


def from_first(shard, axis, index):
    total = jnp.where(index == 0, shard, 0.0)
    for n in range(1, lax.axis_size(axis)):
        total = total + lax.ppermute(shard, axis, [(0, n)])
    return total


def on_device(history, sigma, propagator):
    y1s, y0s, zs, chips, cores = (lax.axis_size(axis) for axis in AXES)
    y1, y0, z, x, core = (lax.axis_index(axis) for axis in AXES)
    mid_index = (y1 * y0s + y0) * zs + z
    mid_count = y1s * y0s * zs
    fin_index = x * cores + core
    slots, cols, _, lanes = history.shape
    assert mid_count == chips * cores * cols and y0s == 2 and cols % 4 == 0

    sigmas = from_everyone(sigma, FIN)

    blocks = from_first(sigma[1:, : STEPS - 1], "z", z)
    blocks = from_first(blocks, ("y1", "y0"), y1 * y0s + y0)

    last = (mid_index == mid_count - 1).astype(jnp.int32)
    common = [mid_index * slots, last, fin_index * cols, mid_index]
    place = lambda pair: jnp.stack([jnp.asarray(n, jnp.int32) for n in common + [pair]])

    half = cols // 2
    pairs = half // 2
    sent = memory_terms(place((1 - y0) * pairs), sigmas, propagator, history, half)
    arrived = lax.ppermute(sent, "y0", [(0, 1), (1, 0)])
    blocks = from_everyone(blocks, FIN)
    own = memory_terms(place(y0 * pairs), sigmas, propagator, history, half)

    terms = recursion(own, arrived, blocks, propagator)
    arrived = lax.all_to_all(terms, MID, 0, 0, tiled=True)
    rows = arrived.reshape(y1s, y0s, zs, STEPS, half, lanes).sum(axis=(0, 2))
    return rows.transpose(1, 0, 2, 3).reshape(STEPS, cols, 1, lanes)


def solution(mesh):
    devices = mesh.devices.reshape(4, 2, 8, 4, 2)
    mesh = Mesh(devices, AXES)
    in_specs = (P(MID, FIN, None, None), P(None, MID, FIN, None), P())
    out_specs = P(None, FIN, MID, None)

    return jax.shard_map(
        on_device, mesh=mesh, in_specs=in_specs, out_specs=out_specs, check_vma=False
    )
```

time: 131 us -> 97.9 us (0.75)
  the two profiles are of different devices: /device:TPU:18 before, /device:TPU:16 now
where the time goes in v1:
time: 97.9 us; the launch traced here: 97.1 us
  starting transfers between devices  36.5 us (37%)
  blocking collectives  32.4 us (33%)
  Pallas kernels  15.5 us (16%)
  local copies, waits for them, and re-layouts  8.67 us (9%)
  waiting for transfers between devices  2.84 us (3%)
    all_to_all x1, blocking collectives, on_device(): arrived = lax.all_to_all(terms, MID, 0, 0, tiled=True)  32.4 us
    ppermute x14, starting transfers between devices, from_first(): total = total + lax.ppermute(shard, axis, [(0, n)])  23.9 us
    pallas_call x2, Pallas kernels, memory_terms(): pl.pallas_call(memory_kernel, grid_spec=pltpu.PrefetchScalarGridSpec(num_...  12.1 us
    all_to_all x2, starting transfers between devices, from_everyone(): lax.all_to_all(jnp.broadcast_to(shard[None], (length, *shard.shape)), axi...  9.1 us
    ppermute x1, starting transfers between devices, on_device(): arrived = lax.ppermute(sent, 'y0', [(0, 1), (1, 0)])  3.47 us
    pallas_call x1, Pallas kernels, recursion(): pl.pallas_call(recursion_kernel, out_shape=jax.ShapeDtypeStruct((orbitals...  3.37 us
    broadcast_in_dim x2, local copies, waits for them, and re-layouts, from_everyone(): jnp.broadcast_to(shard[None], (length, *shard.shape))  3.26 us
    unnamed x6, local copies, waits for them, and re-layouts  2.85 us
  transfers between devices with their start and end apart: 17, of which 3 were waited for; matrix products, arithmetic and copies ran while one was open for 4% of the time, Pallas kernels for 12%

profile of v1, /device:TPU:16, one launch (start us, length us, event | category | flops | bytes accessed | tf_op | source)
XLA Modules:
  0.0 97.1 jit_solution(7185038626105666273)
XLA Ops:
  0.0 2.5 %broadcast_in_dim.9 = f32[8,4,16,8,128]{4,3,2,1,0:T(8,128)} broadcast(f32[4,16,8,128]{3,2,1,0:T(8,128)} %param.4), dimensions={1,2,3,4} | broadcast | bytes 2359296 | tf_op jit(solution)/shard_map/broadcast_in_dim | solution.py:153
  2.5 4.3 %all-to-all-start = ((f32[8,4,16,8,128]{4,3,2,1,0:T(8,128)}), f32[8,4,16,8,128]{4,3,2,1,0:T(8,128)S(1)}, u32[]{:S(2)}, u32[]{:S(2)}) async-start(f32[8,4,16,8,128]{4,3,2,1,0:T(8,128)} %broadcast_in_dim.9), calls=%async_computation | async-start | bytes 4194304 | tf_op jit(solution)/shard_map/all_to_all | solution.py:152
  6.8 0.8 slice.3
  7.6 10.9 %collective-permute-start.7 = (f32[3,3,8,128]{3,2,1,0:T(8,128)S(1)}, f32[3,3,8,128]{3,2,1,0:T(8,128)S(1)}, u32[]{:S(2)}, u32[]{:S(2)}) collective-permute-start(f32[3,3,8,128]{3,2,1,0:T(8,128)S(1)} %slice.3), channel_id=1, source_target_pairs={{0,56},{1,57},{2,58},{3,59},{4,60},{5,61},{6,62},{7,63},{64,120},{... | collective-permute-start | bytes 110600 | tf_op jit(solution)/shard_map/ppermute | solution.py:160
  18.5 1.3 %collective-permute-start.6 = (f32[3,3,8,128]{3,2,1,0:T(8,128)S(1)}, f32[3,3,8,128]{3,2,1,0:T(8,128)S(1)}, u32[]{:S(2)}, u32[]{:S(2)}) collective-permute-start(f32[3,3,8,128]{3,2,1,0:T(8,128)S(1)} %slice.3), channel_id=1, source_target_pairs={{0,48},{1,49},{2,50},{3,51},{4,52},{5,53},{6,54},{7,55},{64,112},{... | collective-permute-start | bytes 110600 | tf_op jit(solution)/shard_map/ppermute | solution.py:160
  19.8 1.3 %collective-permute-start.5 = (f32[3,3,8,128]{3,2,1,0:T(8,128)S(1)}, f32[3,3,8,128]{3,2,1,0:T(8,128)S(1)}, u32[]{:S(2)}, u32[]{:S(2)}) collective-permute-start(f32[3,3,8,128]{3,2,1,0:T(8,128)S(1)} %slice.3), channel_id=1, source_target_pairs={{0,40},{1,41},{2,42},{3,43},{4,44},{5,45},{6,46},{7,47},{64,104},{... | collective-permute-start | bytes 110600 | tf_op jit(solution)/shard_map/ppermute | solution.py:160
  21.1 1.3 %collective-permute-start.4 = (f32[3,3,8,128]{3,2,1,0:T(8,128)S(1)}, f32[3,3,8,128]{3,2,1,0:T(8,128)S(1)}, u32[]{:S(2)}, u32[]{:S(2)}) collective-permute-start(f32[3,3,8,128]{3,2,1,0:T(8,128)S(1)} %slice.3), channel_id=1, source_target_pairs={{0,32},{1,33},{2,34},{3,35},{4,36},{5,37},{6,38},{7,39},{64,96},{6... | collective-permute-start | bytes 110600 | tf_op jit(solution)/shard_map/ppermute | solution.py:160
  22.4 1.3 %collective-permute-start.3 = (f32[3,3,8,128]{3,2,1,0:T(8,128)S(1)}, f32[3,3,8,128]{3,2,1,0:T(8,128)S(1)}, u32[]{:S(2)}, u32[]{:S(2)}) collective-permute-start(f32[3,3,8,128]{3,2,1,0:T(8,128)S(1)} %slice.3), channel_id=1, source_target_pairs={{0,24},{1,25},{2,26},{3,27},{4,28},{5,29},{6,30},{7,31},{64,88},{6... | collective-permute-start | bytes 110600 | tf_op jit(solution)/shard_map/ppermute | solution.py:160
  23.7 0.0 collective-permute-done.7
  23.8 1.3 %collective-permute-start.2 = (f32[3,3,8,128]{3,2,1,0:T(8,128)S(1)}, f32[3,3,8,128]{3,2,1,0:T(8,128)S(1)}, u32[]{:S(2)}, u32[]{:S(2)}) collective-permute-start(f32[3,3,8,128]{3,2,1,0:T(8,128)S(1)} %slice.3), channel_id=1, source_target_pairs={{0,16},{1,17},{2,18},{3,19},{4,20},{5,21},{6,22},{7,23},{64,80},{6... | collective-permute-start | bytes 110600 | tf_op jit(solution)/shard_map/ppermute | solution.py:160
  25.1 0.0 collective-permute-done.6
  25.1 1.3 %collective-permute-start.1 = (f32[3,3,8,128]{3,2,1,0:T(8,128)S(1)}, f32[3,3,8,128]{3,2,1,0:T(8,128)S(1)}, u32[]{:S(2)}, u32[]{:S(2)}) collective-permute-start(f32[3,3,8,128]{3,2,1,0:T(8,128)S(1)} %slice.3), channel_id=1, source_target_pairs={{0,8},{1,9},{2,10},{3,11},{4,12},{5,13},{6,14},{7,15},{64,72},{65,... | collective-permute-start | bytes 110600 | tf_op jit(solution)/shard_map/ppermute | solution.py:160
  26.4 0.0 collective-permute-done.5
  26.4 0.0 collective-permute-done.4
  26.4 0.0 collective-permute-done.3
  26.4 0.3 collective-permute-done.2
  26.7 1.3 %collective-permute-done.1 = f32[3,3,8,128]{3,2,1,0:T(8,128)S(1)} collective-permute-done((f32[3,3,8,128]{3,2,1,0:T(8,128)S(1)}, f32[3,3,8,128]{3,2,1,0:T(8,128)S(1)}, u32[]{:S(2)}, u32[]{:S(2)}) %collective-permute-start.1) | collective-permute-done | bytes 36896 | tf_op jit(solution)/shard_map/ppermute | solution.py:160
  28.0 0.8 add_add_fusion.1
  28.8 0.7 collective-permute-start.14
  29.4 0.7 collective-permute-start.13
  30.1 0.6 stack.39.where_ref
  30.8 0.7 collective-permute-start.12
  31.4 0.7 collective-permute-start.11
  32.1 0.7 collective-permute-start.10
  32.8 0.0 collective-permute-done.14
  32.8 1.3 %collective-permute-start.9 = (f32[3,3,8,128]{3,2,1,0:T(8,128)S(1)}, f32[3,3,8,128]{3,2,1,0:T(8,128)S(1)}, u32[]{:S(2)}, u32[]{:S(2)}) collective-permute-start(f32[3,3,8,128]{3,2,1,0:T(8,128)S(1)} %add_add_fusion.1), channel_id=1, source_target_pairs={{0,128},{1,129},{2,130},{3,131},{4,132},{5,133},{6,134},{7,135},{8... | collective-permute-start | bytes 110600 | tf_op jit(solution)/shard_map/ppermute | solution.py:160
  34.1 0.0 collective-permute-done.13
  34.1 0.7 collective-permute-start.8
  34.7 0.0 all-to-all-done.sigma_ref
  34.8 0.0 copy-start
  34.8 1.3 %copy-done = f32[8,4,16,8,128]{4,3,2,1,0:T(8,128)} copy-done((f32[8,4,16,8,128]{4,3,2,1,0:T(8,128)}, f32[8,4,16,8,128]{4,3,2,1,0:T(8,128)S(1)}, u32[]{:S(2)}) %copy-start) | copy-done | bytes 2097176
  36.1 6.1 %memory_terms.3 = f32[4,4,64,128]{3,2,1,0:T(8,128)} custom-call(s32[5]{0:T(128)} %stack.39.where_ref, f32[8,4,16,8,128]{4,3,2,1,0:T(8,128)} %copy-done, f32[64,128]{1,0:T(8,128)} %propagator_ref.5, f32[16,8,64,128]{3,2,1,0:T(8,128)} %history_ref.3), custom_call_target="tpu_custom_call" | custom-call | flops 1610612736 | bytes 6291456 | tf_op jit(solution)/shard_map/memory_terms/pallas_call | solution.py:84
  42.2 0.0 collective-permute-done.12
  42.2 3.5 %collective-permute-start = (f32[4,4,64,128]{3,2,1,0:T(8,128)}, f32[4,4,64,128]{3,2,1,0:T(8,128)S(1)}, u32[]{:S(2)}, u32[]{:S(2)}) collective-permute-start(f32[4,4,64,128]{3,2,1,0:T(8,128)} %memory_terms.3), channel_id=1, source_target_pairs={{0,64},{64,0},{1,65},{65,1},{2,66},{66,2},{3,67},{67,3},{4,68},{68... | collective-permute-start | bytes 1572872 | tf_op jit(solution)/shard_map/ppermute | solution.py:185
  45.7 0.0 collective-permute-done.11
  45.7 0.0 collective-permute-done.10
  45.7 0.0 collective-permute-done.9
  45.7 0.0 collective-permute-done.8
  45.7 0.7 broadcast_in_dim.19
  46.5 4.8 %all-to-all-start.1 = ((f32[8,3,3,8,128]{4,3,2,1,0:T(8,128)}), f32[8,3,3,8,128]{4,3,2,1,0:T(8,128)S(1)}, u32[]{:S(2)}, u32[]{:S(2)}) async-start(f32[8,3,3,8,128]{4,3,2,1,0:T(8,128)} %broadcast_in_dim.19), calls=%async_computation.1 | async-start | bytes 589824 | tf_op jit(solution)/shard_map/all_to_all | solution.py:152
  51.3 0.6 stack.37.where_ref
  51.8 6.1 %memory_terms.2.own_ref = f32[4,4,64,128]{3,2,1,0:T(8,128)} custom-call(s32[5]{0:T(128)} %stack.37.where_ref, f32[8,4,16,8,128]{4,3,2,1,0:T(8,128)} %copy-done, f32[64,128]{1,0:T(8,128)} %propagator_ref.5, f32[16,8,64,128]{3,2,1,0:T(8,128)} %history_ref.3), custom_call_target="tpu_custom_call" | custom-call | flops 1610612736 | bytes 6291456 | tf_op jit(solution)/shard_map/memory_terms/pallas_call | solution.py:84
  57.9 1.2 %all-to-all-done.1.blocks_ref = f32[8,3,3,8,128]{4,3,2,1,0:T(8,128)S(1)} async-done(((f32[8,3,3,8,128]{4,3,2,1,0:T(8,128)}), f32[8,3,3,8,128]{4,3,2,1,0:T(8,128)S(1)}, u32[]{:S(2)}, u32[]{:S(2)}) %all-to-all-start.1) | async-done | bytes 294944 | tf_op jit(solution)/shard_map/all_to_all | solution.py:152
  59.1 0.0 copy-start.1
  59.1 0.0 collective-permute-done.arrived_ref
  59.1 0.7 copy-done.1
  59.8 0.0 copy-start.2
  59.8 0.8 copy-done.2
  60.6 3.4 %recursion.1 = f32[64,16,128]{2,1,0:T(8,128)} custom-call(f32[4,4,64,128]{3,2,1,0:T(8,128)} %memory_terms.2.own_ref, f32[4,4,64,128]{3,2,1,0:T(8,128)} %copy-done.2, f32[8,3,3,8,128]{4,3,2,1,0:T(8,128)} %copy-done.1, f32[64,128]{1,0:T(8,128)} %propagator_ref.5), custom_call_target="tpu_custom_call" | custom-call | flops 301989888 | bytes 2097152 | tf_op jit(solution)/shard_map/recursion/pallas_call | solution.py:138
  64.0 32.4 %all_to_all.15 = f32[64,16,128]{2,1,0:T(8,128)S(1)} all-to-all(f32[64,16,128]{2,1,0:T(8,128)} %recursion.1), channel_id=1, replica_groups=mesh['y1'=4,'y0'=2,'z'=8,'x'=4,'core'=2] {'y1','y0','z'}, dimensions={0} | all-to-all | bytes 1048576 | tf_op jit(solution)/shard_map/all_to_all | solution.py:190
  96.4 0.1 reduce_sum.9
  96.5 0.6 copy.4
  (1 shorter events, 0.0 us)
Async XLA Ops:
  2.5 32.2 %all-to-all-start = ((f32[8,4,16,8,128]{4,3,2,1,0:T(8,128)}), f32[8,4,16,8,128]{4,3,2,1,0:T(8,128)S(1)}, u32[]{:S(2)}, u32[]{:S(2)}) async-start(f32[8,4,16,8,128]{4,3,2,1,0:T(8,128)} %broadcast_in_dim.9), calls=%async_computation | async-start | bytes 4194304 | tf_op jit(solution)/shard_map/all_to_all | solution.py:152
  7.6 16.1 %collective-permute-start.7 = (f32[3,3,8,128]{3,2,1,0:T(8,128)S(1)}, f32[3,3,8,128]{3,2,1,0:T(8,128)S(1)}, u32[]{:S(2)}, u32[]{:S(2)}) collective-permute-start(f32[3,3,8,128]{3,2,1,0:T(8,128)S(1)} %slice.3), channel_id=1, source_target_pairs={{0,56},{1,57},{2,58},{3,59},{4,60},{5,61},{6,62},{7,63},{64,120},{... | collective-permute-start | bytes 110600 | tf_op jit(solution)/shard_map/ppermute | solution.py:160
  18.5 6.5 %collective-permute-start.6 = (f32[3,3,8,128]{3,2,1,0:T(8,128)S(1)}, f32[3,3,8,128]{3,2,1,0:T(8,128)S(1)}, u32[]{:S(2)}, u32[]{:S(2)}) collective-permute-start(f32[3,3,8,128]{3,2,1,0:T(8,128)S(1)} %slice.3), channel_id=1, source_target_pairs={{0,48},{1,49},{2,50},{3,51},{4,52},{5,53},{6,54},{7,55},{64,112},{... | collective-permute-start | bytes 110600 | tf_op jit(solution)/shard_map/ppermute | solution.py:160
  19.8 6.5 %collective-permute-start.5 = (f32[3,3,8,128]{3,2,1,0:T(8,128)S(1)}, f32[3,3,8,128]{3,2,1,0:T(8,128)S(1)}, u32[]{:S(2)}, u32[]{:S(2)}) collective-permute-start(f32[3,3,8,128]{3,2,1,0:T(8,128)S(1)} %slice.3), channel_id=1, source_target_pairs={{0,40},{1,41},{2,42},{3,43},{4,44},{5,45},{6,46},{7,47},{64,104},{... | collective-permute-start | bytes 110600 | tf_op jit(solution)/shard_map/ppermute | solution.py:160
  21.1 5.2 %collective-permute-start.4 = (f32[3,3,8,128]{3,2,1,0:T(8,128)S(1)}, f32[3,3,8,128]{3,2,1,0:T(8,128)S(1)}, u32[]{:S(2)}, u32[]{:S(2)}) collective-permute-start(f32[3,3,8,128]{3,2,1,0:T(8,128)S(1)} %slice.3), channel_id=1, source_target_pairs={{0,32},{1,33},{2,34},{3,35},{4,36},{5,37},{6,38},{7,39},{64,96},{6... | collective-permute-start | bytes 110600 | tf_op jit(solution)/shard_map/ppermute | solution.py:160
  22.4 4.0 %collective-permute-start.3 = (f32[3,3,8,128]{3,2,1,0:T(8,128)S(1)}, f32[3,3,8,128]{3,2,1,0:T(8,128)S(1)}, u32[]{:S(2)}, u32[]{:S(2)}) collective-permute-start(f32[3,3,8,128]{3,2,1,0:T(8,128)S(1)} %slice.3), channel_id=1, source_target_pairs={{0,24},{1,25},{2,26},{3,27},{4,28},{5,29},{6,30},{7,31},{64,88},{6... | collective-permute-start | bytes 110600 | tf_op jit(solution)/shard_map/ppermute | solution.py:160
  23.8 2.9 %collective-permute-start.2 = (f32[3,3,8,128]{3,2,1,0:T(8,128)S(1)}, f32[3,3,8,128]{3,2,1,0:T(8,128)S(1)}, u32[]{:S(2)}, u32[]{:S(2)}) collective-permute-start(f32[3,3,8,128]{3,2,1,0:T(8,128)S(1)} %slice.3), channel_id=1, source_target_pairs={{0,16},{1,17},{2,18},{3,19},{4,20},{5,21},{6,22},{7,23},{64,80},{6... | collective-permute-start | bytes 110600 | tf_op jit(solution)/shard_map/ppermute | solution.py:160
  25.1 2.9 %collective-permute-start.1 = (f32[3,3,8,128]{3,2,1,0:T(8,128)S(1)}, f32[3,3,8,128]{3,2,1,0:T(8,128)S(1)}, u32[]{:S(2)}, u32[]{:S(2)}) collective-permute-start(f32[3,3,8,128]{3,2,1,0:T(8,128)S(1)} %slice.3), channel_id=1, source_target_pairs={{0,8},{1,9},{2,10},{3,11},{4,12},{5,13},{6,14},{7,15},{64,72},{65,... | collective-permute-start | bytes 110600 | tf_op jit(solution)/shard_map/ppermute | solution.py:160
  28.8 4.0 %collective-permute-start.14 = (f32[3,3,8,128]{3,2,1,0:T(8,128)S(1)}, f32[3,3,8,128]{3,2,1,0:T(8,128)S(1)}, u32[]{:S(2)}, u32[]{:S(2)}) collective-permute-start(f32[3,3,8,128]{3,2,1,0:T(8,128)S(1)} %add_add_fusion.1), channel_id=1, source_target_pairs={{0,448},{1,449},{2,450},{3,451},{4,452},{5,453},{6,454},{7,455},{8... | collective-permute-start | bytes 110600 | tf_op jit(solution)/shard_map/ppermute | solution.py:160
  29.4 4.6 %collective-permute-start.13 = (f32[3,3,8,128]{3,2,1,0:T(8,128)S(1)}, f32[3,3,8,128]{3,2,1,0:T(8,128)S(1)}, u32[]{:S(2)}, u32[]{:S(2)}) collective-permute-start(f32[3,3,8,128]{3,2,1,0:T(8,128)S(1)} %add_add_fusion.1), channel_id=1, source_target_pairs={{0,384},{1,385},{2,386},{3,387},{4,388},{5,389},{6,390},{7,391},{8... | collective-permute-start | bytes 110600 | tf_op jit(solution)/shard_map/ppermute | solution.py:160
  30.8 11.4 %collective-permute-start.12 = (f32[3,3,8,128]{3,2,1,0:T(8,128)S(1)}, f32[3,3,8,128]{3,2,1,0:T(8,128)S(1)}, u32[]{:S(2)}, u32[]{:S(2)}) collective-permute-start(f32[3,3,8,128]{3,2,1,0:T(8,128)S(1)} %add_add_fusion.1), channel_id=1, source_target_pairs={{0,320},{1,321},{2,322},{3,323},{4,324},{5,325},{6,326},{7,327},{8... | collective-permute-start | bytes 110600 | tf_op jit(solution)/shard_map/ppermute | solution.py:160
  31.4 14.3 %collective-permute-start.11 = (f32[3,3,8,128]{3,2,1,0:T(8,128)S(1)}, f32[3,3,8,128]{3,2,1,0:T(8,128)S(1)}, u32[]{:S(2)}, u32[]{:S(2)}) collective-permute-start(f32[3,3,8,128]{3,2,1,0:T(8,128)S(1)} %add_add_fusion.1), channel_id=1, source_target_pairs={{0,256},{1,257},{2,258},{3,259},{4,260},{5,261},{6,262},{7,263},{8... | collective-permute-start | bytes 110600 | tf_op jit(solution)/shard_map/ppermute | solution.py:160
  32.1 13.6 %collective-permute-start.10 = (f32[3,3,8,128]{3,2,1,0:T(8,128)S(1)}, f32[3,3,8,128]{3,2,1,0:T(8,128)S(1)}, u32[]{:S(2)}, u32[]{:S(2)}) collective-permute-start(f32[3,3,8,128]{3,2,1,0:T(8,128)S(1)} %add_add_fusion.1), channel_id=1, source_target_pairs={{0,192},{1,193},{2,194},{3,195},{4,196},{5,197},{6,198},{7,199},{8... | collective-permute-start | bytes 110600 | tf_op jit(solution)/shard_map/ppermute | solution.py:160
  32.8 12.9 %collective-permute-start.9 = (f32[3,3,8,128]{3,2,1,0:T(8,128)S(1)}, f32[3,3,8,128]{3,2,1,0:T(8,128)S(1)}, u32[]{:S(2)}, u32[]{:S(2)}) collective-permute-start(f32[3,3,8,128]{3,2,1,0:T(8,128)S(1)} %add_add_fusion.1), channel_id=1, source_target_pairs={{0,128},{1,129},{2,130},{3,131},{4,132},{5,133},{6,134},{7,135},{8... | collective-permute-start | bytes 110600 | tf_op jit(solution)/shard_map/ppermute | solution.py:160
  34.1 11.6 %collective-permute-start.8 = (f32[3,3,8,128]{3,2,1,0:T(8,128)S(1)}, f32[3,3,8,128]{3,2,1,0:T(8,128)S(1)}, u32[]{:S(2)}, u32[]{:S(2)}) collective-permute-start(f32[3,3,8,128]{3,2,1,0:T(8,128)S(1)} %add_add_fusion.1), channel_id=1, source_target_pairs={{0,64},{1,65},{2,66},{3,67},{4,68},{5,69},{6,70},{7,71},{8,72},{9,... | collective-permute-start | bytes 110600 | tf_op jit(solution)/shard_map/ppermute | solution.py:160
  34.8 1.3 %copy-start = (f32[8,4,16,8,128]{4,3,2,1,0:T(8,128)}, f32[8,4,16,8,128]{4,3,2,1,0:T(8,128)S(1)}, u32[]{:S(2)}) copy-start(f32[8,4,16,8,128]{4,3,2,1,0:T(8,128)S(1)} %all-to-all-done.sigma_ref) | copy-start | bytes 6291460
  42.2 16.9 %collective-permute-start = (f32[4,4,64,128]{3,2,1,0:T(8,128)}, f32[4,4,64,128]{3,2,1,0:T(8,128)S(1)}, u32[]{:S(2)}, u32[]{:S(2)}) collective-permute-start(f32[4,4,64,128]{3,2,1,0:T(8,128)} %memory_terms.3), channel_id=1, source_target_pairs={{0,64},{64,0},{1,65},{65,1},{2,66},{66,2},{3,67},{67,3},{4,68},{68... | collective-permute-start | bytes 1572872 | tf_op jit(solution)/shard_map/ppermute | solution.py:185
  46.5 12.7 %all-to-all-start.1 = ((f32[8,3,3,8,128]{4,3,2,1,0:T(8,128)}), f32[8,3,3,8,128]{4,3,2,1,0:T(8,128)S(1)}, u32[]{:S(2)}, u32[]{:S(2)}) async-start(f32[8,3,3,8,128]{4,3,2,1,0:T(8,128)} %broadcast_in_dim.19), calls=%async_computation.1 | async-start | bytes 589824 | tf_op jit(solution)/shard_map/all_to_all | solution.py:152
  59.1 0.7 copy-start.1
  59.8 0.8 copy-start.2

commit v2 on v1

--- a/solution.py
+++ b/solution.py
@@ -26,37 +26,60 @@
     return jnp.where(lane < half, -rolled, rolled)
 
 
-def memory_kernel(where_ref, sigma_ref, propagator_ref, history_ref, memory_ref, high_ref, low_ref):
+def format_kernel(where_ref, sigma_ref, own_rows_ref, kernels_ref):
+    steps, slots, rows, lanes = sigma_ref.shape
+    half = lanes // 2
+    first_slot, mid_last = where_ref[0], where_ref[1]
+    lane = lax.broadcasted_iota(jnp.int32, (rows, lanes), 1)
+    for k in range(steps):
+        for p in range(0, slots, 2):
+            pair = [sigma_ref[k, p], sigma_ref[k, p + 1]]
+            for q in range(2):
+                if p + q < k:
+                    pair[q] = jnp.where(first_slot + p + q >= k, pair[q], 0.0)
+            if k == 0 and p + 2 == slots:
+                pair[1] = pair[1] + jnp.where(mid_last == 1, own_rows_ref[...], 0.0)
+            real = jnp.where(lane < half, pair[0], pltpu.roll(pair[1], half, 1))
+            imag = jnp.where(lane < half, pltpu.roll(pair[0], half, 1), pair[1])
+            kernels_ref[0, k, 0, :, p * half : p * half + lanes] = real
+            kernels_ref[0, k, 1, :, p * half : p * half + lanes] = imag
+
+
+def formatted(where, sigma, propagator, copies):
+    steps, slots, rows, lanes = sigma.shape
+    block = (1, steps, 2, rows, slots * lanes // 2)
+    return pl.pallas_call(
+        format_kernel,
+        grid_spec=pltpu.PrefetchScalarGridSpec(
+            num_scalar_prefetch=1,
+            grid=(copies,),
+            in_specs=[
+                pl.BlockSpec(sigma.shape, lambda g, w: (0, 0, 0, 0)),
+                pl.BlockSpec((rows, lanes), lambda g, w: (w[2], 0)),
+            ],
+            out_specs=pl.BlockSpec(block, lambda g, w: (g, 0, 0, 0, 0)),
+        ),
+        out_shape=jax.ShapeDtypeStruct((copies, *block[1:]), jnp.float32),
+        compiler_params=pltpu.CompilerParams(dimension_semantics=("arbitrary",)),
+        cost_estimate=pl.CostEstimate(flops=1 << 20, bytes_accessed=2 << 20, transcendentals=0),
+        name="formatted",
+    )(where, sigma, propagator)
+
+
+def memory_kernel(where_ref, same_ref, other_ref, history_ref, memory_ref, high_ref, low_ref):
     step = pl.program_id(0)
-    sources, steps, slots, rows, lanes = sigma_ref.shape
-    half = lanes // 2
-    first_slot, mid_last, first_col, first_device, first_pair = (where_ref[n] for n in range(5))
+    chips, steps, parts, rows, depth = same_ref.shape
+    lanes = history_ref.shape[-1]
+    first_device, first_col, first_pair, core = (where_ref[n] for n in range(4))
+    height = chips * steps * parts * rows
 
     @pl.when(step == 0)
     def _():
-        lane = lax.broadcasted_iota(jnp.int32, (rows, lanes), 1)
-        for n in range(sources):
-            own_rows = propagator_ref[n * rows : (n + 1) * rows, :]
-            own_rows = jnp.where(mid_last == 1, own_rows, 0.0)
-            for k in range(steps):
-                for p in range(0, slots, 2):
-                    pair = [sigma_ref[n, k, p], sigma_ref[n, k, p + 1]]
-                    for q in range(2):
-                        if p + q < k:
-                            pair[q] = jnp.where(first_slot + p + q >= k, pair[q], 0.0)
-                    if k == 0 and p + 2 == slots:
-                        pair[1] = pair[1] + own_rows
-                    real = jnp.where(lane < half, pair[0], pltpu.roll(pair[1], half, 1))
-                    imag = jnp.where(lane < half, pltpu.roll(pair[0], half, 1), pair[1])
-                    high, low = split(jnp.concatenate([real, imag], axis=0))
-                    at = (
-                        pl.ds((n * steps + k) * 2 * rows, 2 * rows),
-                        pl.ds(p * half, lanes),
-                    )
-                    high_ref[at] = high
-                    low_ref[at] = low
-
-    depth = slots * half
+        for n, ref in enumerate((same_ref, other_ref)):
+            high, low = split(ref[...].reshape(height, depth))
+            high_ref[n * height : (n + 1) * height, :] = high
+            low_ref[n * height : (n + 1) * height, :] = low
+
     block = jnp.concatenate(
         [history_ref[:, c].reshape(depth, lanes) for c in range(2)], axis=1
     )
@@ -65,21 +88,23 @@
     total = dot(high_ref[...], block_high) + (
         dot(low_ref[...], block_high) + dot(high_ref[...], block_low)
     )
-    total = total.reshape(sources, steps, 2, rows, 2 * lanes)
+    total = total.reshape(2, chips, steps, parts, rows, 2 * lanes)
     for c in range(2):
         column = total[..., c * lanes : (c + 1) * lanes]
-        value = column[:, :, 0] + turn(column[:, :, 1])
+        value = column[:, :, :, 0] + turn(column[:, :, :, 1])
         kept = first_device >= first_col + 2 * (first_pair + step) + c
         value = jnp.where(kept, value, 0.0)
-        for k in range(steps):
-            memory_ref[c, k] = value[:, k].reshape(sources * rows, lanes)
-
-
-def memory_terms(where, sigma, propagator, history, cols):
-    sources, steps, _, rows, _ = sigma.shape
+        for n in range(2):
+            owner = core if n == 0 else 1 - core
+            for chip in range(chips):
+                row = pl.multiple_of((2 * chip + owner) * rows, rows)
+                memory_ref[c, :, pl.ds(row, rows), :] = value[n, chip]
+
+
+def memory_terms(where, same, other, history, cols):
+    chips, steps, parts, rows, depth = same.shape
     slots, _, orbitals, lanes = history.shape
-    height = sources * steps * 2 * rows
-    depth = slots * orbitals
+    height = 2 * chips * steps * parts * rows
     whole = lambda array: pl.BlockSpec(array.shape, lambda g, w: (0,) * array.ndim)
     return pl.pallas_call(
         memory_kernel,
@@ -87,9 +112,9 @@
             num_scalar_prefetch=1,
             grid=(cols // 2,),
             in_specs=[
-                whole(sigma),
-                whole(propagator),
-                pl.BlockSpec((slots, 2, orbitals, lanes), lambda g, w: (0, w[4] + g, 0, 0)),
+                whole(same),
+                whole(other),
+                pl.BlockSpec((slots, 2, orbitals, lanes), lambda g, w: (0, w[2] + g, 0, 0)),
             ],
             out_specs=pl.BlockSpec((2, steps, orbitals, lanes), lambda g, w: (g, 0, 0, 0)),
             scratch_shapes=[pltpu.VMEM((height, depth), jnp.bfloat16)] * 2,
@@ -102,7 +127,7 @@
             transcendentals=0,
         ),
         name="memory_terms",
-    )(where, sigma, propagator, history)
+    )(where, same, other, history)
 
 
 def recursion_kernel(own_ref, arrived_ref, blocks_ref, propagator_ref, out_ref):
@@ -170,21 +195,23 @@
     slots, cols, _, lanes = history.shape
     assert mid_count == chips * cores * cols and y0s == 2 and cols % 4 == 0
 
-    sigmas = from_everyone(sigma, FIN)
+    table = lambda *entries: jnp.stack([jnp.asarray(n, jnp.int32) for n in entries])
+    last = (mid_index == mid_count - 1).astype(jnp.int32)
+
+    kernels = formatted(table(mid_index * slots, last, fin_index), sigma, propagator, chips)
+    same = lax.all_to_all(kernels, "x", 0, 0, tiled=True)
+    other = lax.ppermute(same, "core", [(0, 1), (1, 0)])
 
     blocks = from_first(sigma[1:, : STEPS - 1], "z", z)
-    blocks = from_first(blocks, ("y1", "y0"), y1 * y0s + y0)
-
-    last = (mid_index == mid_count - 1).astype(jnp.int32)
-    common = [mid_index * slots, last, fin_index * cols, mid_index]
-    place = lambda pair: jnp.stack([jnp.asarray(n, jnp.int32) for n in common + [pair]])
+    blocks = from_everyone(blocks, ("y1", "y0"))[0]
 
     half = cols // 2
     pairs = half // 2
-    sent = memory_terms(place((1 - y0) * pairs), sigmas, propagator, history, half)
+    place = lambda pair: table(mid_index, fin_index * cols, pair, core)
+    sent = memory_terms(place((1 - y0) * pairs), same, other, history, half)
     arrived = lax.ppermute(sent, "y0", [(0, 1), (1, 0)])
     blocks = from_everyone(blocks, FIN)
-    own = memory_terms(place(y0 * pairs), sigmas, propagator, history, half)
+    own = memory_terms(place(y0 * pairs), same, other, history, half)
 
     terms = recursion(own, arrived, blocks, propagator)
     arrived = lax.all_to_all(terms, MID, 0, 0, tiled=True)

time: 97.9 us -> 112 us (1.14)
  blocking collectives: 32.4 us -> 47 us
  local copies, waits for them, and re-layouts: 8.67 us -> 5.42 us
  Pallas kernels: 15.5 us -> 18.3 us
  other arithmetic: 0.91 us -> 2.79 us
  starting transfers between devices: 36.5 us -> 34.8 us
    all_to_all x0 -> x1, blocking collectives: none -> 19.4 us  [on_device(): same = lax.all_to_all(kernels, 'x', 0, 0, tiled=True)]
    ppermute x14 -> x7, starting transfers between devices: 23.9 us -> 18.7 us  [from_first(): total = total + lax.ppermute(shard, axis, [(0, n)])]
    all_to_all x1, blocking collectives: 32.4 us -> 27.6 us  [on_device(): arrived = lax.all_to_all(terms, MID, 0, 0, tiled=True)]
    pallas_call x0 -> x1, Pallas kernels: none -> 3.48 us  [formatted(): pl.pallas_call(format_kernel, grid_spec=pltpu.PrefetchScalarGridSpec(num_...]
    ppermute x0 -> x1, starting transfers between devices: none -> 1.91 us  [on_device(): other = lax.ppermute(same, 'core', [(0, 1), (1, 0)])]
    another operation x0 -> x3, other arithmetic: none -> 1.9 us  [on_device(): jnp.stack([jnp.asarray(n, jnp.int32) for n in entries])]
    broadcast_in_dim x2 -> x3, local copies, waits for them, and re-layouts: 3.26 us -> 1.5 us  [from_everyone(): jnp.broadcast_to(shard[None], (length, *shard.shape))]
    all_to_all x2, starting transfers between devices: 9.1 us -> 10.9 us  [from_everyone(): lax.all_to_all(jnp.broadcast_to(shard[None], (length, *shard.shape)), axi...]
  transfers between devices with their start and end apart: 17 -> 11, of which waited for: 3 -> 3; matrix products, arithmetic and copies ran while one was open for 4% -> 4% of each run, Pallas kernels for 12% -> 10%
where the time goes in v2:
time: 112 us; the launch traced here: 111 us
  blocking collectives  47 us (42%)
  starting transfers between devices  34.8 us (31%)
  Pallas kernels  18.3 us (16%)
  local copies, waits for them, and re-layouts  5.42 us (5%)
  waiting for transfers between devices  3 us (3%)
  other arithmetic  2.79 us (2%)
    all_to_all x1, blocking collectives, on_device(): arrived = lax.all_to_all(terms, MID, 0, 0, tiled=True)  27.6 us
    all_to_all x1, blocking collectives, on_device(): same = lax.all_to_all(kernels, 'x', 0, 0, tiled=True)  19.4 us
    ppermute x7, starting transfers between devices, from_first(): total = total + lax.ppermute(shard, axis, [(0, n)])  18.7 us
    pallas_call x2, Pallas kernels, memory_terms(): pl.pallas_call(memory_kernel, grid_spec=pltpu.PrefetchScalarGridSpec(num_...  11.4 us
    all_to_all x2, starting transfers between devices, from_everyone(): lax.all_to_all(jnp.broadcast_to(shard[None], (length, *shard.shape)), axi...  10.9 us
    pallas_call x1, Pallas kernels, formatted(): pl.pallas_call(format_kernel, grid_spec=pltpu.PrefetchScalarGridSpec(num_...  3.48 us
    pallas_call x1, Pallas kernels, recursion(): pl.pallas_call(recursion_kernel, out_shape=jax.ShapeDtypeStruct((orbitals...  3.36 us
    ppermute x1, starting transfers between devices, on_device(): arrived = lax.ppermute(sent, 'y0', [(0, 1), (1, 0)])  3.36 us
  transfers between devices with their start and end apart: 11, of which 3 were waited for; matrix products, arithmetic and copies ran while one was open for 4% of the time, Pallas kernels for 10%

profile of v2, /device:TPU:16, one launch (start us, length us, event | category | flops | bytes accessed | tf_op | source)
XLA Modules:
  0.0 111.5 jit_solution(5941065186338373457)
XLA Ops:
  0.0 0.7 pad_add_fusion.1.where_ref
  0.7 3.5 %formatted.1 = f32[4,4,2,8,1024]{4,3,2,1,0:T(8,128)} custom-call(s32[3]{0:T(128)} %pad_add_fusion.1.where_ref, f32[4,16,8,128]{3,2,1,0:T(8,128)} %sigma_ref.1, f32[64,128]{1,0:T(8,128)} %propagator_ref.1), custom_call_target="tpu_custom_call" | custom-call | flops 1048576 | bytes 2097152 | tf_op jit(solution)/shard_map/formatted/pallas_call | solution.py:51
  4.2 19.4 %all_to_all.20.same_ref = f32[4,4,2,8,1024]{4,3,2,1,0:T(8,128)S(1)} all-to-all(f32[4,4,2,8,1024]{4,3,2,1,0:T(8,128)} %formatted.1), channel_id=1, replica_groups=mesh['y1'=4,'y0'=2,'z'=8,'x'=4,'core'=2] {'x'}, dimensions={0} | all-to-all | bytes 2097152 | tf_op jit(solution)/shard_map/all_to_all | solution.py:202
  23.5 0.0 copy-start
  23.5 1.9 %collective-permute-start = (f32[4,4,2,8,1024]{4,3,2,1,0:T(8,128)S(1)}, f32[4,4,2,8,1024]{4,3,2,1,0:T(8,128)S(1)}, u32[]{:S(2)}, u32[]{:S(2)}) collective-permute-start(f32[4,4,2,8,1024]{4,3,2,1,0:T(8,128)S(1)} %all_to_all.20.same_ref), channel_id=1, source_target_pairs={{0,1},{1,0},{2,3},{3,2},{4,5},{5,4},{6,7},{7,6},{8,9},{9,8},{10,11... | collective-permute-start | bytes 3145736 | tf_op jit(solution)/shard_map/ppermute | solution.py:203
  25.5 0.8 slice.6
  26.2 10.9 %collective-permute-start.8 = (f32[3,3,8,128]{3,2,1,0:T(8,128)S(1)}, f32[3,3,8,128]{3,2,1,0:T(8,128)S(1)}, u32[]{:S(2)}, u32[]{:S(2)}) collective-permute-start(f32[3,3,8,128]{3,2,1,0:T(8,128)S(1)} %slice.6), channel_id=1, source_target_pairs={{0,56},{1,57},{2,58},{3,59},{4,60},{5,61},{6,62},{7,63},{64,120},{... | collective-permute-start | bytes 110600 | tf_op jit(solution)/shard_map/ppermute | solution.py:185
  37.2 1.3 %collective-permute-start.7 = (f32[3,3,8,128]{3,2,1,0:T(8,128)S(1)}, f32[3,3,8,128]{3,2,1,0:T(8,128)S(1)}, u32[]{:S(2)}, u32[]{:S(2)}) collective-permute-start(f32[3,3,8,128]{3,2,1,0:T(8,128)S(1)} %slice.6), channel_id=1, source_target_pairs={{0,48},{1,49},{2,50},{3,51},{4,52},{5,53},{6,54},{7,55},{64,112},{... | collective-permute-start | bytes 110600 | tf_op jit(solution)/shard_map/ppermute | solution.py:185
  38.5 1.3 %collective-permute-start.6 = (f32[3,3,8,128]{3,2,1,0:T(8,128)S(1)}, f32[3,3,8,128]{3,2,1,0:T(8,128)S(1)}, u32[]{:S(2)}, u32[]{:S(2)}) collective-permute-start(f32[3,3,8,128]{3,2,1,0:T(8,128)S(1)} %slice.6), channel_id=1, source_target_pairs={{0,40},{1,41},{2,42},{3,43},{4,44},{5,45},{6,46},{7,47},{64,104},{... | collective-permute-start | bytes 110600 | tf_op jit(solution)/shard_map/ppermute | solution.py:185
  39.8 1.3 %collective-permute-start.5 = (f32[3,3,8,128]{3,2,1,0:T(8,128)S(1)}, f32[3,3,8,128]{3,2,1,0:T(8,128)S(1)}, u32[]{:S(2)}, u32[]{:S(2)}) collective-permute-start(f32[3,3,8,128]{3,2,1,0:T(8,128)S(1)} %slice.6), channel_id=1, source_target_pairs={{0,32},{1,33},{2,34},{3,35},{4,36},{5,37},{6,38},{7,39},{64,96},{6... | collective-permute-start | bytes 110600 | tf_op jit(solution)/shard_map/ppermute | solution.py:185
  41.1 0.0 collective-permute-done.8
  41.1 1.3 %collective-permute-start.4 = (f32[3,3,8,128]{3,2,1,0:T(8,128)S(1)}, f32[3,3,8,128]{3,2,1,0:T(8,128)S(1)}, u32[]{:S(2)}, u32[]{:S(2)}) collective-permute-start(f32[3,3,8,128]{3,2,1,0:T(8,128)S(1)} %slice.6), channel_id=1, source_target_pairs={{0,24},{1,25},{2,26},{3,27},{4,28},{5,29},{6,30},{7,31},{64,88},{6... | collective-permute-start | bytes 110600 | tf_op jit(solution)/shard_map/ppermute | solution.py:185
  42.4 0.0 collective-permute-done.7
  42.4 1.3 %collective-permute-start.3 = (f32[3,3,8,128]{3,2,1,0:T(8,128)S(1)}, f32[3,3,8,128]{3,2,1,0:T(8,128)S(1)}, u32[]{:S(2)}, u32[]{:S(2)}) collective-permute-start(f32[3,3,8,128]{3,2,1,0:T(8,128)S(1)} %slice.6), channel_id=1, source_target_pairs={{0,16},{1,17},{2,18},{3,19},{4,20},{5,21},{6,22},{7,23},{64,80},{6... | collective-permute-start | bytes 110600 | tf_op jit(solution)/shard_map/ppermute | solution.py:185
  43.7 0.0 collective-permute-done.6
  43.7 1.3 %collective-permute-start.2 = (f32[3,3,8,128]{3,2,1,0:T(8,128)S(1)}, f32[3,3,8,128]{3,2,1,0:T(8,128)S(1)}, u32[]{:S(2)}, u32[]{:S(2)}) collective-permute-start(f32[3,3,8,128]{3,2,1,0:T(8,128)S(1)} %slice.6), channel_id=1, source_target_pairs={{0,8},{1,9},{2,10},{3,11},{4,12},{5,13},{6,14},{7,15},{64,72},{65,... | collective-permute-start | bytes 110600 | tf_op jit(solution)/shard_map/ppermute | solution.py:185
  45.0 0.0 collective-permute-done.5
  45.0 0.0 collective-permute-done.4
  45.0 0.3 collective-permute-done.3
  45.3 1.3 %collective-permute-done.2 = f32[3,3,8,128]{3,2,1,0:T(8,128)S(1)} collective-permute-done((f32[3,3,8,128]{3,2,1,0:T(8,128)S(1)}, f32[3,3,8,128]{3,2,1,0:T(8,128)S(1)}, u32[]{:S(2)}, u32[]{:S(2)}) %collective-permute-start.2) | collective-permute-done | bytes 36896 | tf_op jit(solution)/shard_map/ppermute | solution.py:185
  46.6 0.8 add_add_fusion
  47.4 0.8 broadcast_in_dim.18
  48.2 7.4 %all-to-all-start.1 = ((f32[8,3,3,8,128]{4,3,2,1,0:T(8,128)}), f32[8,3,3,8,128]{4,3,2,1,0:T(8,128)S(1)}, u32[]{:S(2)}, u32[]{:S(2)}) async-start(f32[8,3,3,8,128]{4,3,2,1,0:T(8,128)} %broadcast_in_dim.18), calls=%async_computation.1 | async-start | bytes 589824 | tf_op jit(solution)/shard_map/all_to_all | solution.py:177
  55.6 0.6 add_add_fusion.2.where_ref
  56.2 0.0 collective-permute-done.other_ref
  56.2 0.0 copy-done
  56.2 0.0 copy-start.1
  56.2 1.0 copy-done.1
  57.2 5.7 %memory_terms.3 = f32[4,4,64,128]{3,2,1,0:T(8,128)} custom-call(s32[4]{0:T(128)} %add_add_fusion.2.where_ref, f32[4,4,2,8,1024]{4,3,2,1,0:T(8,128)} %copy-done, f32[4,4,2,8,1024]{4,3,2,1,0:T(8,128)} %copy-done.1, f32[16,8,64,128]{3,2,1,0:T(8,128)} %history_ref.3), custom_call_target="tpu_custom_call" | custom-call | flops 1610612736 | bytes 6291456 | tf_op jit(solution)/shard_map/memory_terms/pallas_call | solution.py:109
  62.9 3.4 %collective-permute-start.1 = (f32[4,4,64,128]{3,2,1,0:T(8,128)}, f32[4,4,64,128]{3,2,1,0:T(8,128)S(1)}, u32[]{:S(2)}, u32[]{:S(2)}) collective-permute-start(f32[4,4,64,128]{3,2,1,0:T(8,128)} %memory_terms.3), channel_id=1, source_target_pairs={{0,64},{64,0},{1,65},{65,1},{2,66},{66,2},{3,67},{67,3},{4,68},{68... | collective-permute-start | bytes 1572872 | tf_op jit(solution)/shard_map/ppermute | solution.py:212
  66.3 0.0 all-to-all-done.1
  66.3 0.7 broadcast_in_dim.20
  67.0 3.4 %all-to-all-start.2 = ((f32[8,3,3,8,128]{4,3,2,1,0:T(8,128)}), f32[8,3,3,8,128]{4,3,2,1,0:T(8,128)S(1)}, u32[]{:S(2)}, u32[]{:S(2)}) async-start(f32[8,3,3,8,128]{4,3,2,1,0:T(8,128)} %broadcast_in_dim.20), calls=%async_computation.2 | async-start | bytes 589824 | tf_op jit(solution)/shard_map/all_to_all | solution.py:177
  70.4 0.7 add_add_fusion.1.where_ref
  71.1 5.7 %memory_terms.2.own_ref = f32[4,4,64,128]{3,2,1,0:T(8,128)} custom-call(s32[4]{0:T(128)} %add_add_fusion.1.where_ref, f32[4,4,2,8,1024]{4,3,2,1,0:T(8,128)} %copy-done, f32[4,4,2,8,1024]{4,3,2,1,0:T(8,128)} %copy-done.1, f32[16,8,64,128]{3,2,1,0:T(8,128)} %history_ref.3), custom_call_target="tpu_custom_call" | custom-call | flops 1610612736 | bytes 6291456 | tf_op jit(solution)/shard_map/memory_terms/pallas_call | solution.py:109
  76.8 1.4 %all-to-all-done.2.blocks_ref = f32[8,3,3,8,128]{4,3,2,1,0:T(8,128)S(1)} async-done(((f32[8,3,3,8,128]{4,3,2,1,0:T(8,128)}), f32[8,3,3,8,128]{4,3,2,1,0:T(8,128)S(1)}, u32[]{:S(2)}, u32[]{:S(2)}) %all-to-all-start.2) | async-done | bytes 294944 | tf_op jit(solution)/shard_map/all_to_all | solution.py:177
  78.2 0.0 copy-start.2
  78.2 0.0 collective-permute-done.1.arrived_ref
  78.2 0.7 copy-done.2
  79.0 0.0 copy-start.3
  79.0 0.8 copy-done.3
  79.8 3.4 %recursion.1 = f32[64,16,128]{2,1,0:T(8,128)} custom-call(f32[4,4,64,128]{3,2,1,0:T(8,128)} %memory_terms.2.own_ref, f32[4,4,64,128]{3,2,1,0:T(8,128)} %copy-done.3, f32[8,3,3,8,128]{4,3,2,1,0:T(8,128)} %copy-done.2, f32[64,128]{1,0:T(8,128)} %propagator_ref.1), custom_call_target="tpu_custom_call" | custom-call | flops 301989888 | bytes 2097152 | tf_op jit(solution)/shard_map/recursion/pallas_call | solution.py:163
  83.1 27.6 %all_to_all.21 = f32[64,16,128]{2,1,0:T(8,128)S(1)} all-to-all(f32[64,16,128]{2,1,0:T(8,128)} %recursion.1), channel_id=1, replica_groups=mesh['y1'=4,'y0'=2,'z'=8,'x'=4,'core'=2] {'y1','y0','z'}, dimensions={0} | all-to-all | bytes 1048576 | tf_op jit(solution)/shard_map/all_to_all | solution.py:217
  110.7 0.1 reduce_sum.9
  110.8 0.6 copy.4
  (1 shorter events, 0.0 us)
Async XLA Ops:
  23.5 32.6 %copy-start = (f32[4,4,2,8,1024]{4,3,2,1,0:T(8,128)}, f32[4,4,2,8,1024]{4,3,2,1,0:T(8,128)S(1)}, u32[]{:S(2)}) copy-start(f32[4,4,2,8,1024]{4,3,2,1,0:T(8,128)S(1)} %all_to_all.20.same_ref) | copy-start | bytes 3145732
  23.5 32.6 %collective-permute-start = (f32[4,4,2,8,1024]{4,3,2,1,0:T(8,128)S(1)}, f32[4,4,2,8,1024]{4,3,2,1,0:T(8,128)S(1)}, u32[]{:S(2)}, u32[]{:S(2)}) collective-permute-start(f32[4,4,2,8,1024]{4,3,2,1,0:T(8,128)S(1)} %all_to_all.20.same_ref), channel_id=1, source_target_pairs={{0,1},{1,0},{2,3},{3,2},{4,5},{5,4},{6,7},{7,6},{8,9},{9,8},{10,11... | collective-permute-start | bytes 3145736 | tf_op jit(solution)/shard_map/ppermute | solution.py:203
  26.2 14.8 %collective-permute-start.8 = (f32[3,3,8,128]{3,2,1,0:T(8,128)S(1)}, f32[3,3,8,128]{3,2,1,0:T(8,128)S(1)}, u32[]{:S(2)}, u32[]{:S(2)}) collective-permute-start(f32[3,3,8,128]{3,2,1,0:T(8,128)S(1)} %slice.6), channel_id=1, source_target_pairs={{0,56},{1,57},{2,58},{3,59},{4,60},{5,61},{6,62},{7,63},{64,120},{... | collective-permute-start | bytes 110600 | tf_op jit(solution)/shard_map/ppermute | solution.py:185
  37.2 5.2 %collective-permute-start.7 = (f32[3,3,8,128]{3,2,1,0:T(8,128)S(1)}, f32[3,3,8,128]{3,2,1,0:T(8,128)S(1)}, u32[]{:S(2)}, u32[]{:S(2)}) collective-permute-start(f32[3,3,8,128]{3,2,1,0:T(8,128)S(1)} %slice.6), channel_id=1, source_target_pairs={{0,48},{1,49},{2,50},{3,51},{4,52},{5,53},{6,54},{7,55},{64,112},{... | collective-permute-start | bytes 110600 | tf_op jit(solution)/shard_map/ppermute | solution.py:185
  38.5 5.2 %collective-permute-start.6 = (f32[3,3,8,128]{3,2,1,0:T(8,128)S(1)}, f32[3,3,8,128]{3,2,1,0:T(8,128)S(1)}, u32[]{:S(2)}, u32[]{:S(2)}) collective-permute-start(f32[3,3,8,128]{3,2,1,0:T(8,128)S(1)} %slice.6), channel_id=1, source_target_pairs={{0,40},{1,41},{2,42},{3,43},{4,44},{5,45},{6,46},{7,47},{64,104},{... | collective-permute-start | bytes 110600 | tf_op jit(solution)/shard_map/ppermute | solution.py:185
  39.8 5.2 %collective-permute-start.5 = (f32[3,3,8,128]{3,2,1,0:T(8,128)S(1)}, f32[3,3,8,128]{3,2,1,0:T(8,128)S(1)}, u32[]{:S(2)}, u32[]{:S(2)}) collective-permute-start(f32[3,3,8,128]{3,2,1,0:T(8,128)S(1)} %slice.6), channel_id=1, source_target_pairs={{0,32},{1,33},{2,34},{3,35},{4,36},{5,37},{6,38},{7,39},{64,96},{6... | collective-permute-start | bytes 110600 | tf_op jit(solution)/shard_map/ppermute | solution.py:185
  41.1 3.9 %collective-permute-start.4 = (f32[3,3,8,128]{3,2,1,0:T(8,128)S(1)}, f32[3,3,8,128]{3,2,1,0:T(8,128)S(1)}, u32[]{:S(2)}, u32[]{:S(2)}) collective-permute-start(f32[3,3,8,128]{3,2,1,0:T(8,128)S(1)} %slice.6), channel_id=1, source_target_pairs={{0,24},{1,25},{2,26},{3,27},{4,28},{5,29},{6,30},{7,31},{64,88},{6... | collective-permute-start | bytes 110600 | tf_op jit(solution)/shard_map/ppermute | solution.py:185
  42.4 2.9 %collective-permute-start.3 = (f32[3,3,8,128]{3,2,1,0:T(8,128)S(1)}, f32[3,3,8,128]{3,2,1,0:T(8,128)S(1)}, u32[]{:S(2)}, u32[]{:S(2)}) collective-permute-start(f32[3,3,8,128]{3,2,1,0:T(8,128)S(1)} %slice.6), channel_id=1, source_target_pairs={{0,16},{1,17},{2,18},{3,19},{4,20},{5,21},{6,22},{7,23},{64,80},{6... | collective-permute-start | bytes 110600 | tf_op jit(solution)/shard_map/ppermute | solution.py:185
  43.7 2.9 %collective-permute-start.2 = (f32[3,3,8,128]{3,2,1,0:T(8,128)S(1)}, f32[3,3,8,128]{3,2,1,0:T(8,128)S(1)}, u32[]{:S(2)}, u32[]{:S(2)}) collective-permute-start(f32[3,3,8,128]{3,2,1,0:T(8,128)S(1)} %slice.6), channel_id=1, source_target_pairs={{0,8},{1,9},{2,10},{3,11},{4,12},{5,13},{6,14},{7,15},{64,72},{65,... | collective-permute-start | bytes 110600 | tf_op jit(solution)/shard_map/ppermute | solution.py:185
  48.2 18.1 %all-to-all-start.1 = ((f32[8,3,3,8,128]{4,3,2,1,0:T(8,128)}), f32[8,3,3,8,128]{4,3,2,1,0:T(8,128)S(1)}, u32[]{:S(2)}, u32[]{:S(2)}) async-start(f32[8,3,3,8,128]{4,3,2,1,0:T(8,128)} %broadcast_in_dim.18), calls=%async_computation.1 | async-start | bytes 589824 | tf_op jit(solution)/shard_map/all_to_all | solution.py:177
  56.2 1.0 copy-start.1
  62.9 15.3 %collective-permute-start.1 = (f32[4,4,64,128]{3,2,1,0:T(8,128)}, f32[4,4,64,128]{3,2,1,0:T(8,128)S(1)}, u32[]{:S(2)}, u32[]{:S(2)}) collective-permute-start(f32[4,4,64,128]{3,2,1,0:T(8,128)} %memory_terms.3), channel_id=1, source_target_pairs={{0,64},{64,0},{1,65},{65,1},{2,66},{66,2},{3,67},{67,3},{4,68},{68... | collective-permute-start | bytes 1572872 | tf_op jit(solution)/shard_map/ppermute | solution.py:212
  67.0 11.2 %all-to-all-start.2 = ((f32[8,3,3,8,128]{4,3,2,1,0:T(8,128)}), f32[8,3,3,8,128]{4,3,2,1,0:T(8,128)S(1)}, u32[]{:S(2)}, u32[]{:S(2)}) async-start(f32[8,3,3,8,128]{4,3,2,1,0:T(8,128)} %broadcast_in_dim.20), calls=%async_computation.2 | async-start | bytes 589824 | tf_op jit(solution)/shard_map/all_to_all | solution.py:177
  78.2 0.7 copy-start.2
  79.0 0.8 copy-start.3

commit v3 on v1

v3 whole, which is shorter than its diff:
```python
import jax
import jax.numpy as jnp
from jax import lax
from jax.experimental import pallas as pl
from jax.experimental.pallas import tpu as pltpu
from jax.sharding import Mesh, PartitionSpec as P


STEPS = 4
AXES = ("y1", "y0", "z", "x", "core")
MID, FIN = AXES[:3], AXES[3:]


def split(value):
    high = value.astype(jnp.bfloat16)
    low = (value - high.astype(jnp.float32)).astype(jnp.bfloat16)
    return high, low


def turn(block):
    lanes = block.shape[-1]
    half = lanes // 2
    rolled = pltpu.roll(block, half, block.ndim - 1)
    lane = lax.broadcasted_iota(jnp.int32, block.shape, block.ndim - 1)
    return jnp.where(lane < half, -rolled, rolled)


def in_vmem(array):
    return pltpu.with_memory_space_constraint(array, pltpu.VMEM)


def dot(a, b):
    return jnp.dot(a, b, preferred_element_type=jnp.float32)


def memory_kernel(where_ref, *refs):
    sigma_refs, (propagator_ref, history_ref, sent_ref, own_ref, high_ref, low_ref) = refs[:2], refs[2:]
    step = pl.program_id(0)
    chips, steps, slots, rows, lanes = sigma_refs[0].shape
    half = lanes // 2
    first_slot, mid_last, first_device, first_col, core, y0 = (where_ref[n] for n in range(6))

    def source_row(n, chip):
        owner = core if n == 0 else 1 - core
        return pl.multiple_of((2 * chip + owner) * rows, rows)

    @pl.when(step == 0)
    def _():
        lane = lax.broadcasted_iota(jnp.int32, (rows, lanes), 1)
        for n, ref in enumerate(sigma_refs):
            for chip in range(chips):
                own_rows = propagator_ref[pl.ds(source_row(n, chip), rows), :]
                own_rows = jnp.where(mid_last == 1, own_rows, 0.0)
                for k in range(steps):
                    for p in range(0, slots, 2):
                        pair = [ref[chip, k, p], ref[chip, k, p + 1]]
                        for q in range(2):
                            if p + q < k:
                                pair[q] = jnp.where(first_slot + p + q >= k, pair[q], 0.0)
                        if k == 0 and p + 2 == slots:
                            pair[1] = pair[1] + own_rows
                        real = jnp.where(lane < half, pair[0], pltpu.roll(pair[1], half, 1))
                        imag = jnp.where(lane < half, pltpu.roll(pair[0], half, 1), pair[1])
                        high, low = split(jnp.concatenate([real, imag], axis=0))
                        at = (
                            pl.ds(((n * chips + chip) * steps + k) * 2 * rows, 2 * rows),
                            pl.ds(p * half, lanes),
                        )
                        high_ref[at] = high
                        low_ref[at] = low

    depth = slots * half
    block = jnp.concatenate(
        [history_ref[:, c].reshape(depth, lanes) for c in range(2)], axis=1
    )
    block_high, block_low = split(block)
    total = dot(high_ref[...], block_high) + (
        dot(low_ref[...], block_high) + dot(high_ref[...], block_low)
    )
    total = total.reshape(2, chips, steps, 2, rows, 2 * lanes)
    pairs = pl.num_programs(0)
    first_pair = lax.rem(step + pairs // 2 * (1 - y0), pairs)

    def store(memory_ref):
        for c in range(2):
            column = total[..., c * lanes : (c + 1) * lanes]
            value = column[:, :, :, 0] + turn(column[:, :, :, 1])
            kept = first_device >= first_col + 2 * first_pair + c
            value = jnp.where(kept, value, 0.0)
            for n in range(2):
                for chip in range(chips):
                    memory_ref[c, :, pl.ds(source_row(n, chip), rows), :] = value[n, chip]

    @pl.when(step < pairs // 2)
    def _():
        store(sent_ref)

    @pl.when(step >= pairs // 2)
    def _():
        store(own_ref)


def memory_terms(where, same, other, propagator, history):
    chips, steps, slots, rows, lanes = same.shape
    _, cols, orbitals, _ = history.shape
    height = 2 * chips * steps * 2 * rows
    depth = slots * orbitals
    pairs = cols // 2
    whole = lambda array: pl.BlockSpec(array.shape, lambda g, w: (0,) * array.ndim)
    pair = lambda g, w: lax.rem(g + pairs // 2 * (1 - w[5]), pairs)
    block = (2, steps, orbitals, lanes)
    shape = jax.ShapeDtypeStruct((cols // 2, steps, orbitals, lanes), jnp.float32)
    return pl.pallas_call(
        memory_kernel,
        grid_spec=pltpu.PrefetchScalarGridSpec(
            num_scalar_prefetch=1,
            grid=(pairs,),
            in_specs=[
                pl.BlockSpec(memory_space=pltpu.VMEM),
                pl.BlockSpec(memory_space=pltpu.VMEM),
                whole(propagator),
                pl.BlockSpec((slots, 2, orbitals, lanes), lambda g, w: (0, pair(g, w), 0, 0)),
            ],
            out_specs=[
                pl.BlockSpec(block, lambda g, w: (jnp.minimum(g, pairs // 2 - 1), 0, 0, 0)),
                pl.BlockSpec(block, lambda g, w: (jnp.maximum(g - pairs // 2, 0), 0, 0, 0)),
            ],
            scratch_shapes=[pltpu.VMEM((height, depth), jnp.bfloat16)] * 2,
        ),
        out_shape=[shape, shape],
        compiler_params=pltpu.CompilerParams(dimension_semantics=("arbitrary",)),
        cost_estimate=pl.CostEstimate(
            flops=6 * height * depth * cols * lanes,
            bytes_accessed=8 << 20,
            transcendentals=0,
        ),
        name="memory_terms",
    )(where, *(in_vmem(array) for array in (same, other)), propagator, history)


def recursion_kernel(own_ref, arrived_ref, blocks_ref, propagator_ref, out_ref):
    cols, steps, orbitals, lanes = own_ref.shape
    stacked_high, stacked_low = [], []
    for k in range(steps):
        columns = [own_ref[c, k] + arrived_ref[c, k] for c in range(cols)]
        if k:
            weights = []
            for l in range(k):
                weight = blocks_ref[:, k - 1, l].reshape(orbitals, lanes)
                if l == k - 1:
                    weight = weight + propagator_ref[...]
                weights.append(weight)
            high, low = split(jnp.concatenate(weights, axis=1))
            update = dot(high, jnp.concatenate(stacked_high, axis=0)) + (
                dot(low, jnp.concatenate(stacked_high, axis=0))
                + dot(high, jnp.concatenate(stacked_low, axis=0))
            )
            columns = [
                columns[c] + update[:, c * lanes : (c + 1) * lanes] for c in range(cols)
            ]
        if k < steps - 1:
            for part in (columns, [turn(column) for column in columns]):
                high, low = split(jnp.concatenate(part, axis=1))
                stacked_high.append(high)
                stacked_low.append(low)
        for c in range(cols):
            out_ref[:, k * cols + c, :] = columns[c]


def recursion(own, arrived, blocks, propagator):
    cols, steps, orbitals, lanes = own.shape
    return pl.pallas_call(
        recursion_kernel,
        out_shape=jax.ShapeDtypeStruct((orbitals, steps * cols, lanes), jnp.float32),
        in_specs=[pl.BlockSpec(memory_space=pltpu.VMEM)] * 4,
        cost_estimate=pl.CostEstimate(
            flops=12 * 6 * orbitals * 2 * orbitals * cols * lanes,
            bytes_accessed=2 << 20,
            transcendentals=0,
        ),
        name="recursion",
    )(own, in_vmem(arrived), in_vmem(blocks), propagator)


def from_everyone(shard, axis):
    length = lax.axis_size(axis)
    return lax.all_to_all(
        jnp.broadcast_to(shard[None], (length, *shard.shape)), axis, 0, 0, tiled=True
    )


def from_first(shard, axis, index):
    total = jnp.where(index == 0, shard, 0.0)
    for n in range(1, lax.axis_size(axis)):
        total = total + lax.ppermute(shard, axis, [(0, n)])
    return total


def on_device(history, sigma, propagator):
    y1s, y0s, zs, chips, cores = (lax.axis_size(axis) for axis in AXES)
    y1, y0, z, x, core = (lax.axis_index(axis) for axis in AXES)
    mid_index = (y1 * y0s + y0) * zs + z
    mid_count = y1s * y0s * zs
    fin_index = x * cores + core
    slots, cols, _, lanes = history.shape
    assert mid_count == chips * cores * cols and y0s == 2 and cols % 4 == 0

    same = from_everyone(sigma, "x")
    other = lax.ppermute(same, "core", [(0, 1), (1, 0)])

    blocks = from_first(sigma[1:, : STEPS - 1], "z", z)
    blocks = from_everyone(blocks, ("y1", "y0"))[0]

    last = (mid_index == mid_count - 1).astype(jnp.int32)
    where = [mid_index * slots, last, mid_index, fin_index * cols, core, y0]
    where = jnp.stack([jnp.asarray(n, jnp.int32) for n in where])
    sent, own = memory_terms(where, same, other, propagator, history)
    arrived = lax.ppermute(sent, "y0", [(0, 1), (1, 0)])
    blocks = from_everyone(blocks, FIN)

    terms = recursion(own, arrived, blocks, propagator)
    arrived = lax.all_to_all(terms, MID, 0, 0, tiled=True)
    rows = arrived.reshape(y1s, y0s, zs, STEPS, cols // 2, lanes).sum(axis=(0, 2))
    return rows.transpose(1, 0, 2, 3).reshape(STEPS, cols, 1, lanes)


def solution(mesh):
    devices = mesh.devices.reshape(4, 2, 8, 4, 2)
    mesh = Mesh(devices, AXES)
    in_specs = (P(MID, FIN, None, None), P(None, MID, FIN, None), P())
    out_specs = P(None, FIN, MID, None)

    return jax.shard_map(
        on_device, mesh=mesh, in_specs=in_specs, out_specs=out_specs, check_vma=False
    )
```

time: 97.9 us -> 107 us (1.093)
  blocking collectives: 32.4 us -> 57.4 us
  starting transfers between devices: 36.5 us -> 29.5 us
  local copies, waits for them, and re-layouts: 8.67 us -> 3.87 us
  Pallas kernels: 15.5 us -> 11 us
    all_to_all x0 -> x2, blocking collectives: none -> 29.4 us  [from_everyone(): lax.all_to_all(jnp.broadcast_to(shard[None], (length, *shard.shape)), axi...]
    ppermute x14 -> x7, starting transfers between devices: 23.9 us -> 16.8 us  [from_first(): total = total + lax.ppermute(shard, axis, [(0, n)])]
    all_to_all x1, blocking collectives: 32.4 us -> 28 us  [on_device(): arrived = lax.all_to_all(terms, MID, 0, 0, tiled=True)]
    pallas_call x2 -> x1, Pallas kernels: 12.1 us -> 8.08 us  [memory_terms(): pl.pallas_call(memory_kernel, grid_spec=pltpu.PrefetchScalarGridSpec(num_...]
    unnamed x6 -> x0, local copies, waits for them, and re-layouts: 2.85 us -> none
    ppermute x0 -> x1, starting transfers between devices: none -> 1.91 us  [on_device(): other = lax.ppermute(same, 'core', [(0, 1), (1, 0)])]
    all_to_all x2 -> x1, starting transfers between devices: 9.1 us -> 7.43 us  [from_everyone(): lax.all_to_all(jnp.broadcast_to(shard[None], (length, *shard.shape)), axi...]
    broadcast_in_dim x2 -> x4, local copies, waits for them, and re-layouts: 3.26 us -> 1.82 us  [from_everyone(): jnp.broadcast_to(shard[None], (length, *shard.shape))]
  transfers between devices with their start and end apart: 17 -> 10, of which waited for: 3 -> 3; matrix products, arithmetic and copies ran while one was open for 4% -> 3% of each run, Pallas kernels for 12% -> 8%
where the time goes in v3:
time: 107 us; the launch traced here: 106 us
  blocking collectives  57.4 us (54%)
  starting transfers between devices  29.5 us (28%)
  Pallas kernels  11 us (10%)
  local copies, waits for them, and re-layouts  3.87 us (4%)
  waiting for transfers between devices  2.96 us (3%)
    all_to_all x2, blocking collectives, from_everyone(): lax.all_to_all(jnp.broadcast_to(shard[None], (length, *shard.shape)), axi...  29.4 us
    all_to_all x1, blocking collectives, on_device(): arrived = lax.all_to_all(terms, MID, 0, 0, tiled=True)  28 us
    ppermute x7, starting transfers between devices, from_first(): total = total + lax.ppermute(shard, axis, [(0, n)])  16.8 us
    pallas_call x1, Pallas kernels, memory_terms(): pl.pallas_call(memory_kernel, grid_spec=pltpu.PrefetchScalarGridSpec(num_...  8.08 us
    all_to_all x1, starting transfers between devices, from_everyone(): lax.all_to_all(jnp.broadcast_to(shard[None], (length, *shard.shape)), axi...  7.43 us
    ppermute x1, starting transfers between devices, on_device(): arrived = lax.ppermute(sent, 'y0', [(0, 1), (1, 0)])  3.36 us
    pallas_call x1, Pallas kernels, recursion(): pl.pallas_call(recursion_kernel, out_shape=jax.ShapeDtypeStruct((orbitals...  2.96 us
  transfers between devices with their start and end apart: 10, of which 3 were waited for; matrix products, arithmetic and copies ran while one was open for 3% of the time, Pallas kernels for 8%

profile of v3, /device:TPU:16, one launch (start us, length us, event | category | flops | bytes accessed | tf_op | source)
XLA Modules:
  0.0 105.8 jit_solution(16708049787116491712)
XLA Ops:
  0.0 1.0 broadcast_in_dim.12
  1.1 19.2 %all_to_all.20.refs_0_ = f32[4,4,16,8,128]{4,3,2,1,0:T(8,128)S(1)} all-to-all(f32[4,4,16,8,128]{4,3,2,1,0:T(8,128)S(1)} %broadcast_in_dim.12), channel_id=1, replica_groups=mesh['y1'=4,'y0'=2,'z'=8,'x'=4,'core'=2] {'x'}, dimensions={0} | all-to-all | bytes 2097152 | tf_op jit(solution)/shard_map/all_to_all | solution.py:187
  20.2 1.9 %collective-permute-start = (f32[4,4,16,8,128]{4,3,2,1,0:T(8,128)S(1)}, f32[4,4,16,8,128]{4,3,2,1,0:T(8,128)S(1)}, u32[]{:S(2)}, u32[]{:S(2)}) collective-permute-start(f32[4,4,16,8,128]{4,3,2,1,0:T(8,128)S(1)} %all_to_all.20.refs_0_), channel_id=1, source_target_pairs={{0,1},{1,0},{2,3},{3,2},{4,5},{5,4},{6,7},{7,6},{8,9},{9,8},{10,11... | collective-permute-start | bytes 3145736 | tf_op jit(solution)/shard_map/ppermute | solution.py:209
  22.2 0.8 slice.6
  22.9 4.3 %collective-permute-start.2 = (f32[3,3,8,128]{3,2,1,0:T(8,128)S(1)}, f32[3,3,8,128]{3,2,1,0:T(8,128)S(1)}, u32[]{:S(2)}, u32[]{:S(2)}) collective-permute-start(f32[3,3,8,128]{3,2,1,0:T(8,128)S(1)} %slice.6), channel_id=1, source_target_pairs={{0,8},{1,9},{2,10},{3,11},{4,12},{5,13},{6,14},{7,15},{64,72},{65,... | collective-permute-start | bytes 110600 | tf_op jit(solution)/shard_map/ppermute | solution.py:195
  27.2 2.5 %collective-permute-start.3 = (f32[3,3,8,128]{3,2,1,0:T(8,128)S(1)}, f32[3,3,8,128]{3,2,1,0:T(8,128)S(1)}, u32[]{:S(2)}, u32[]{:S(2)}) collective-permute-start(f32[3,3,8,128]{3,2,1,0:T(8,128)S(1)} %slice.6), channel_id=1, source_target_pairs={{0,16},{1,17},{2,18},{3,19},{4,20},{5,21},{6,22},{7,23},{64,80},{6... | collective-permute-start | bytes 110600 | tf_op jit(solution)/shard_map/ppermute | solution.py:195
  29.7 2.5 %collective-permute-start.4 = (f32[3,3,8,128]{3,2,1,0:T(8,128)S(1)}, f32[3,3,8,128]{3,2,1,0:T(8,128)S(1)}, u32[]{:S(2)}, u32[]{:S(2)}) collective-permute-start(f32[3,3,8,128]{3,2,1,0:T(8,128)S(1)} %slice.6), channel_id=1, source_target_pairs={{0,24},{1,25},{2,26},{3,27},{4,28},{5,29},{6,30},{7,31},{64,88},{6... | collective-permute-start | bytes 110600 | tf_op jit(solution)/shard_map/ppermute | solution.py:195
  32.2 3.7 %collective-permute-start.5 = (f32[3,3,8,128]{3,2,1,0:T(8,128)S(1)}, f32[3,3,8,128]{3,2,1,0:T(8,128)S(1)}, u32[]{:S(2)}, u32[]{:S(2)}) collective-permute-start(f32[3,3,8,128]{3,2,1,0:T(8,128)S(1)} %slice.6), channel_id=1, source_target_pairs={{0,32},{1,33},{2,34},{3,35},{4,36},{5,37},{6,38},{7,39},{64,96},{6... | collective-permute-start | bytes 110600 | tf_op jit(solution)/shard_map/ppermute | solution.py:195
  35.9 0.0 collective-permute-done.2
  35.9 1.3 %collective-permute-start.6 = (f32[3,3,8,128]{3,2,1,0:T(8,128)S(1)}, f32[3,3,8,128]{3,2,1,0:T(8,128)S(1)}, u32[]{:S(2)}, u32[]{:S(2)}) collective-permute-start(f32[3,3,8,128]{3,2,1,0:T(8,128)S(1)} %slice.6), channel_id=1, source_target_pairs={{0,40},{1,41},{2,42},{3,43},{4,44},{5,45},{6,46},{7,47},{64,104},{... | collective-permute-start | bytes 110600 | tf_op jit(solution)/shard_map/ppermute | solution.py:195
  37.2 0.0 collective-permute-done.3
  37.2 1.3 %collective-permute-start.7 = (f32[3,3,8,128]{3,2,1,0:T(8,128)S(1)}, f32[3,3,8,128]{3,2,1,0:T(8,128)S(1)}, u32[]{:S(2)}, u32[]{:S(2)}) collective-permute-start(f32[3,3,8,128]{3,2,1,0:T(8,128)S(1)} %slice.6), channel_id=1, source_target_pairs={{0,48},{1,49},{2,50},{3,51},{4,52},{5,53},{6,54},{7,55},{64,112},{... | collective-permute-start | bytes 110600 | tf_op jit(solution)/shard_map/ppermute | solution.py:195
  38.5 0.0 collective-permute-done.4
  38.5 1.3 %collective-permute-start.8 = (f32[3,3,8,128]{3,2,1,0:T(8,128)S(1)}, f32[3,3,8,128]{3,2,1,0:T(8,128)S(1)}, u32[]{:S(2)}, u32[]{:S(2)}) collective-permute-start(f32[3,3,8,128]{3,2,1,0:T(8,128)S(1)} %slice.6), channel_id=1, source_target_pairs={{0,56},{1,57},{2,58},{3,59},{4,60},{5,61},{6,62},{7,63},{64,120},{... | collective-permute-start | bytes 110600 | tf_op jit(solution)/shard_map/ppermute | solution.py:195
  39.8 0.0 collective-permute-done.5
  39.8 0.0 collective-permute-done.6
  39.8 0.3 collective-permute-done.7
  40.1 1.3 %collective-permute-done.8 = f32[3,3,8,128]{3,2,1,0:T(8,128)S(1)} collective-permute-done((f32[3,3,8,128]{3,2,1,0:T(8,128)S(1)}, f32[3,3,8,128]{3,2,1,0:T(8,128)S(1)}, u32[]{:S(2)}, u32[]{:S(2)}) %collective-permute-start.8) | collective-permute-done | bytes 36896 | tf_op jit(solution)/shard_map/ppermute | solution.py:195
  41.4 0.8 add_add_fusion
  42.2 0.7 broadcast_in_dim.25
  43.0 7.4 %all-to-all-start.1 = ((f32[8,3,3,8,128]{4,3,2,1,0:T(8,128)}), f32[8,3,3,8,128]{4,3,2,1,0:T(8,128)S(1)}, u32[]{:S(2)}, u32[]{:S(2)}) async-start(f32[8,3,3,8,128]{4,3,2,1,0:T(8,128)} %broadcast_in_dim.25), calls=%async_computation.1 | async-start | bytes 589824 | tf_op jit(solution)/shard_map/all_to_all | solution.py:187
  50.4 0.7 stack.31.where_ref
  51.0 0.0 collective-permute-done.refs_1_
  51.0 8.1 %memory_terms.1 = (f32[4,4,64,128]{3,2,1,0:T(8,128)}, f32[4,4,64,128]{3,2,1,0:T(8,128)}) custom-call(s32[6]{0:T(128)} %stack.31.where_ref, f32[4,4,16,8,128]{4,3,2,1,0:T(8,128)S(1)} %all_to_all.20.refs_0_, f32[4,4,16,8,128]{4,3,2,1,0:T(8,128)S(1)} %collective-permute-done.refs_1_, f32[64,128]{1,0:T(8,128)} %propagator_ref.1, f32[16,8,64,128]{3,2,1,0:T(8,128)} %refs_3_.1), custom_call_target="tpu_custom_call" | custom-call | flops 3221225472 | bytes 8388608 | tf_op jit(solution)/shard_map/memory_terms/pallas_call | solution.py:113
  59.1 3.4 %collective-permute-start.1 = (f32[4,4,64,128]{3,2,1,0:T(8,128)}, f32[4,4,64,128]{3,2,1,0:T(8,128)S(1)}, u32[]{:S(2)}, u32[]{:S(2)}) collective-permute-start(f32[4,4,64,128]{3,2,1,0:T(8,128)} %get-tuple-element.8), channel_id=1, source_target_pairs={{0,64},{64,0},{1,65},{65,1},{2,66},{66,2},{3,67},{67,3},{4,68},{68... | collective-permute-start | bytes 1572872 | tf_op jit(solution)/shard_map/ppermute | solution.py:218
  62.5 0.0 all-to-all-done.1
  62.6 10.2 %all_to_all.21.blocks_ref = f32[8,3,3,8,128]{4,3,2,1,0:T(8,128)S(1)} all-to-all(f32[8,3,3,8,128]{4,3,2,1,0:T(8,128)S(1)} %broadcast_in_dim.27), channel_id=1, replica_groups=mesh['y1'=4,'y0'=2,'z'=8,'x'=4,'core'=2] {'x','core'}, dimensions={0} | all-to-all | bytes 589824 | tf_op jit(solution)/shard_map/all_to_all | solution.py:187
  72.8 1.4 %collective-permute-done.1.arrived_ref = f32[4,4,64,128]{3,2,1,0:T(8,128)S(1)} collective-permute-done((f32[4,4,64,128]{3,2,1,0:T(8,128)}, f32[4,4,64,128]{3,2,1,0:T(8,128)S(1)}, u32[]{:S(2)}, u32[]{:S(2)}) %collective-permute-start.1) | collective-permute-done | bytes 524320 | tf_op jit(solution)/shard_map/ppermute | solution.py:218
  74.1 3.0 %recursion.1 = f32[64,16,128]{2,1,0:T(8,128)} custom-call(f32[4,4,64,128]{3,2,1,0:T(8,128)} %get-tuple-element.7.own_ref, f32[4,4,64,128]{3,2,1,0:T(8,128)S(1)} %collective-permute-done.1.arrived_ref, f32[8,3,3,8,128]{4,3,2,1,0:T(8,128)S(1)} %all_to_all.21.blocks_ref, f32[64,128]{1,0:T(8,128)} %propagator_ref.1), custom_call_target="tpu_custom_call" | custom-call | flops 301989888 | bytes 2097152 | tf_op jit(solution)/shard_map/recursion/pallas_call | solution.py:172
  77.1 28.0 %all_to_all.22 = f32[64,16,128]{2,1,0:T(8,128)S(1)} all-to-all(f32[64,16,128]{2,1,0:T(8,128)} %recursion.1), channel_id=1, replica_groups=mesh['y1'=4,'y0'=2,'z'=8,'x'=4,'core'=2] {'y1','y0','z'}, dimensions={0} | all-to-all | bytes 1048576 | tf_op jit(solution)/shard_map/all_to_all | solution.py:222
  105.1 0.1 reduce_sum.9
  105.2 0.6 copy.4
  (2 shorter events, 0.0 us)
Async XLA Ops:
  20.2 30.8 %collective-permute-start = (f32[4,4,16,8,128]{4,3,2,1,0:T(8,128)S(1)}, f32[4,4,16,8,128]{4,3,2,1,0:T(8,128)S(1)}, u32[]{:S(2)}, u32[]{:S(2)}) collective-permute-start(f32[4,4,16,8,128]{4,3,2,1,0:T(8,128)S(1)} %all_to_all.20.refs_0_), channel_id=1, source_target_pairs={{0,1},{1,0},{2,3},{3,2},{4,5},{5,4},{6,7},{7,6},{8,9},{9,8},{10,11... | collective-permute-start | bytes 3145736 | tf_op jit(solution)/shard_map/ppermute | solution.py:209
  22.9 12.9 %collective-permute-start.2 = (f32[3,3,8,128]{3,2,1,0:T(8,128)S(1)}, f32[3,3,8,128]{3,2,1,0:T(8,128)S(1)}, u32[]{:S(2)}, u32[]{:S(2)}) collective-permute-start(f32[3,3,8,128]{3,2,1,0:T(8,128)S(1)} %slice.6), channel_id=1, source_target_pairs={{0,8},{1,9},{2,10},{3,11},{4,12},{5,13},{6,14},{7,15},{64,72},{65,... | collective-permute-start | bytes 110600 | tf_op jit(solution)/shard_map/ppermute | solution.py:195
  27.2 10.0 %collective-permute-start.3 = (f32[3,3,8,128]{3,2,1,0:T(8,128)S(1)}, f32[3,3,8,128]{3,2,1,0:T(8,128)S(1)}, u32[]{:S(2)}, u32[]{:S(2)}) collective-permute-start(f32[3,3,8,128]{3,2,1,0:T(8,128)S(1)} %slice.6), channel_id=1, source_target_pairs={{0,16},{1,17},{2,18},{3,19},{4,20},{5,21},{6,22},{7,23},{64,80},{6... | collective-permute-start | bytes 110600 | tf_op jit(solution)/shard_map/ppermute | solution.py:195
  29.7 8.8 %collective-permute-start.4 = (f32[3,3,8,128]{3,2,1,0:T(8,128)S(1)}, f32[3,3,8,128]{3,2,1,0:T(8,128)S(1)}, u32[]{:S(2)}, u32[]{:S(2)}) collective-permute-start(f32[3,3,8,128]{3,2,1,0:T(8,128)S(1)} %slice.6), channel_id=1, source_target_pairs={{0,24},{1,25},{2,26},{3,27},{4,28},{5,29},{6,30},{7,31},{64,88},{6... | collective-permute-start | bytes 110600 | tf_op jit(solution)/shard_map/ppermute | solution.py:195
  32.2 7.6 %collective-permute-start.5 = (f32[3,3,8,128]{3,2,1,0:T(8,128)S(1)}, f32[3,3,8,128]{3,2,1,0:T(8,128)S(1)}, u32[]{:S(2)}, u32[]{:S(2)}) collective-permute-start(f32[3,3,8,128]{3,2,1,0:T(8,128)S(1)} %slice.6), channel_id=1, source_target_pairs={{0,32},{1,33},{2,34},{3,35},{4,36},{5,37},{6,38},{7,39},{64,96},{6... | collective-permute-start | bytes 110600 | tf_op jit(solution)/shard_map/ppermute | solution.py:195
  35.9 3.9 %collective-permute-start.6 = (f32[3,3,8,128]{3,2,1,0:T(8,128)S(1)}, f32[3,3,8,128]{3,2,1,0:T(8,128)S(1)}, u32[]{:S(2)}, u32[]{:S(2)}) collective-permute-start(f32[3,3,8,128]{3,2,1,0:T(8,128)S(1)} %slice.6), channel_id=1, source_target_pairs={{0,40},{1,41},{2,42},{3,43},{4,44},{5,45},{6,46},{7,47},{64,104},{... | collective-permute-start | bytes 110600 | tf_op jit(solution)/shard_map/ppermute | solution.py:195
  37.2 2.9 %collective-permute-start.7 = (f32[3,3,8,128]{3,2,1,0:T(8,128)S(1)}, f32[3,3,8,128]{3,2,1,0:T(8,128)S(1)}, u32[]{:S(2)}, u32[]{:S(2)}) collective-permute-start(f32[3,3,8,128]{3,2,1,0:T(8,128)S(1)} %slice.6), channel_id=1, source_target_pairs={{0,48},{1,49},{2,50},{3,51},{4,52},{5,53},{6,54},{7,55},{64,112},{... | collective-permute-start | bytes 110600 | tf_op jit(solution)/shard_map/ppermute | solution.py:195
  38.5 2.9 %collective-permute-start.8 = (f32[3,3,8,128]{3,2,1,0:T(8,128)S(1)}, f32[3,3,8,128]{3,2,1,0:T(8,128)S(1)}, u32[]{:S(2)}, u32[]{:S(2)}) collective-permute-start(f32[3,3,8,128]{3,2,1,0:T(8,128)S(1)} %slice.6), channel_id=1, source_target_pairs={{0,56},{1,57},{2,58},{3,59},{4,60},{5,61},{6,62},{7,63},{64,120},{... | collective-permute-start | bytes 110600 | tf_op jit(solution)/shard_map/ppermute | solution.py:195
  43.0 19.6 %all-to-all-start.1 = ((f32[8,3,3,8,128]{4,3,2,1,0:T(8,128)}), f32[8,3,3,8,128]{4,3,2,1,0:T(8,128)S(1)}, u32[]{:S(2)}, u32[]{:S(2)}) async-start(f32[8,3,3,8,128]{4,3,2,1,0:T(8,128)} %broadcast_in_dim.25), calls=%async_computation.1 | async-start | bytes 589824 | tf_op jit(solution)/shard_map/all_to_all | solution.py:187
  59.1 15.0 %collective-permute-start.1 = (f32[4,4,64,128]{3,2,1,0:T(8,128)}, f32[4,4,64,128]{3,2,1,0:T(8,128)S(1)}, u32[]{:S(2)}, u32[]{:S(2)}) collective-permute-start(f32[4,4,64,128]{3,2,1,0:T(8,128)} %get-tuple-element.8), channel_id=1, source_target_pairs={{0,64},{64,0},{1,65},{65,1},{2,66},{66,2},{3,67},{67,3},{4,68},{68... | collective-permute-start | bytes 1572872 | tf_op jit(solution)/shard_map/ppermute | solution.py:218
